TPU v7x, 32 devices: a whole 2x2x4 slice. The times are simulated.
32 devices in a mesh: lvl: 2 (over core), front: 4 (over z), grid: 4 (over y, x).
Axes of the slice: x: 2, y: 2, z: 4, core: 2. Of those that a mesh axis runs over, the one named last changes fastest.
Arguments:
- child_panel: bfloat16 [4, 2, 4, 2, 128, 512], P('front', None, 'grid', 'lvl'), may hold values from -0.6 to 0.6
- child_blocks: int32 [4], P('front'), may hold values from 6 to 8, as said below
- tile_rows: int32 [2, 4, 4, 64], P('lvl', 'front', 'grid'), may hold values from 0 to 1
- tile_cols: int32 [2, 4, 4, 64], P('lvl', 'front', 'grid'), may hold values from 0 to 7
- tile_parent: int32 [2, 4, 4, 64, 1], P('lvl', 'front', 'grid'), may hold values from 0 to 3; in each aligned block of 64 rows (0 to 63, 64 to 127, ..., all dimensions but the last counted through in order) at most 32 rows name the same one
- tile_place: int32 [2, 4, 4, 64], P('lvl', 'front', 'grid'), may hold values from 0 to 15
- parent_owner: int32 [4], replicated, may hold values from 0 to 3, each once
- parent_front: float32 [4, 2, 4, 2, 128, 2048], P('front', None, 'grid', 'lvl'), may hold values from -1.5 to 151.5, as said below
Outputs:
- factored: float32 [4, 2, 4, 2, 128, 2048], P('front', None, 'grid', 'lvl')
Inputs may be any that keep to these rules, and one draw needn't show every extreme that they name: `child_blocks`: some child front has exactly 8 blocks. `tile_parent`: among the 64 tiles of one device at most 32 name the same parent front, and some parent front is named by exactly 32. `parent_owner`: each front index holds exactly one parent. `parent_front`: the diagonal of each parent's first diagonal block lies between 148.5 and 151.5; all other entries lie within -1.5 to 1.5.
All inputs are finite; a program needn't handle non-finite values.
Results may differ from a plain program's by a relative error of at most 0.00053.
Values may be sent and summed in bfloat16 or wider, within the bound.
A program may use at most 64 MiB of HBM per device.

v0:
```python
import jax
import jax.numpy as jnp
from jax import lax
from jax.sharding import PartitionSpec as P

BLOCK = 256


def broadcast(block, axis, source):
    block = jnp.where(lax.axis_index(axis) == source, block, jnp.zeros_like(block))
    return lax.psum(block, axis)


def per_device(
    child_panel,
    child_blocks,
    tile_rows,
    tile_cols,
    tile_parent,
    tile_place,
    parent_owner,
    parent_front,
):
    level_count = lax.axis_size("lvl")
    grid_count = lax.axis_size("grid")
    front_count = lax.axis_size("front")
    grid_index = lax.axis_index("grid")
    child_local = child_panel.shape[1]
    half_rows = child_panel.shape[4]
    panel_width = child_panel.shape[5]
    parent_local = parent_front.shape[1]
    front_width = parent_front.shape[5]
    block_count = front_width // BLOCK
    slot_count = tile_rows.shape[3]
    capacity = 2 * slot_count // front_count
    slot_total = front_count * capacity
    own_rows = child_panel.reshape(child_local, half_rows, panel_width)
    gathered = lax.all_gather(
        own_rows.reshape(1, child_local, half_rows, panel_width),
        ("lvl", "grid"),
        axis=0,
        tiled=True,
    )
    panel_view = gathered.reshape(level_count, grid_count, child_local, half_rows, panel_width)
    row_local = tile_rows.reshape(slot_count)
    col_block = tile_cols.reshape(slot_count)
    col_grid = col_block % grid_count
    col_local = col_block // grid_count

    def tile_group(indices):

        def one_tile(row_pick, grid_pick, local_pick):
            left_rows = own_rows[row_pick]
            right_rows = panel_view[:, grid_pick, local_pick].reshape(BLOCK, panel_width)
            product = jnp.einsum(
                "ik,jk->ij", left_rows, right_rows, preferred_element_type=jnp.float32
            )
            return (-product).astype(jnp.bfloat16)

        return jax.vmap(one_tile)(indices[0], indices[1], indices[2])

    grouped = (
        jnp.stack([row_local, col_grid, col_local])
        .reshape(3, 8, slot_count // 8)
        .transpose(1, 0, 2)
    )
    update_tiles = lax.map(tile_group, grouped).reshape(slot_count, half_rows, BLOCK)
    child_size = child_blocks[0]
    live_tile = (row_local * grid_count + grid_index < child_size) & (col_block < child_size)
    update_tiles = jnp.where(live_tile[:, None, None], update_tiles, jnp.zeros((), jnp.bfloat16))
    parents = tile_parent.reshape(slot_count)
    places = tile_place.reshape(slot_count)
    front_ids = jnp.arange(front_count, dtype=jnp.int32)
    owners = jnp.sum(
        jnp.where(parents[:, None] == front_ids[None, :], parent_owner[None, :], 0), axis=1
    )
    one_hot = (owners[:, None] == front_ids[None, :]).astype(jnp.int32)
    rank_within = jnp.sum((jnp.cumsum(one_hot, axis=0) - 1) * one_hot, axis=1)
    slot_index = owners * capacity + rank_within
    matches = slot_index[None, :] == jnp.arange(slot_total, dtype=jnp.int32)[:, None]
    filled = jnp.any(matches, axis=1)
    source = jnp.sum(
        jnp.where(matches, jnp.arange(slot_count, dtype=jnp.int32)[None, :], 0), axis=1
    )
    outgoing = jnp.where(filled[:, None, None], update_tiles[source], jnp.zeros((), jnp.bfloat16))
    positions = jnp.where(filled, places[source], -1)
    incoming, landed = (
        lax.all_to_all(outgoing, "front", split_axis=0, concat_axis=0, tiled=True),
        lax.all_to_all(positions, "front", split_axis=0, concat_axis=0, tiled=True),
    )
    spots = parent_local * block_count
    selector = (landed[:, None] == jnp.arange(spots, dtype=jnp.int32)[None, :]).astype(jnp.bfloat16)
    contrib = jnp.einsum("sk,sij->kij", selector, incoming, preferred_element_type=jnp.float32)
    contrib = (
        contrib.reshape(parent_local, block_count, half_rows, BLOCK)
        .transpose(0, 2, 1, 3)
        .reshape(parent_local, half_rows, front_width)
    )
    assembled = parent_front.reshape(parent_local, half_rows, front_width) + contrib
    own_half = assembled[0, :, :BLOCK]
    joined = lax.all_gather(own_half, "lvl", axis=0, tiled=True)
    pivot_block = broadcast(joined, "grid", 0)
    pivot_block = 0.5 * (pivot_block + pivot_block.T)
    lower_factor = jnp.linalg.cholesky(pivot_block)
    first_column = assembled[:, :, :BLOCK].reshape(parent_local * half_rows, BLOCK)
    panel_rows = lax.linalg.triangular_solve(
        lower_factor, first_column, left_side=False, lower=True, transpose_a=True
    )
    panel_rows = panel_rows.reshape(parent_local, half_rows, BLOCK)
    shared = lax.all_gather(
        panel_rows.reshape(1, parent_local, half_rows, BLOCK), ("lvl", "grid"), axis=0, tiled=True
    )
    shared = shared.reshape(level_count, grid_count, parent_local, half_rows, BLOCK)
    schur = jnp.einsum("rik,lgsjk->risglj", panel_rows, shared, precision=lax.Precision.HIGHEST)
    schur = schur.reshape(parent_local, half_rows, front_width)
    trailing = assembled[:, :, BLOCK:] - schur[:, :, BLOCK:]
    result = jnp.concatenate([panel_rows, trailing], axis=2)
    return result.reshape(1, parent_local, 1, 1, half_rows, front_width)


def solution(mesh):
    return jax.shard_map(
        per_device,
        mesh=mesh,
        in_specs=(
            P("front", None, "grid", "lvl", None, None),
            P("front"),
            P("lvl", "front", "grid", None),
            P("lvl", "front", "grid", None),
            P("lvl", "front", "grid", None, None),
            P("lvl", "front", "grid", None),
            P(),
            P("front", None, "grid", "lvl", None, None),
        ),
        out_specs=P("front", None, "grid", "lvl", None, None),
        check_vma=False,
    )
```

profile of v0, /device:TPU:9, one launch (start us, length us, event | category | flops | bytes accessed | tf_op | source)
XLA Modules:
  0.0 449.1 jit_solution(15282769628164825725)
XLA Ops:
  7.3 0.8 select_reduce_fusion.4
  8.6 1.2 gather_fusion.2
  10.6 4.8 %all-to-all-start = ((s32[4,32,1]{1,2,0:T(1,128)}), s32[4,32,1]{1,2,0:T(1,128)S(1)}, u32[]{:S(2)}, u32[]{:S(2)}) async-start(s32[4,32,1]{1,2,0:T(1,128)} %bitcast.12), calls=%async_computation | async-start | bytes 4096 | tf_op jit(solution)/shard_map/all_to_all | solution.py:89
  15.9 1.3 reduce.21
  17.3 1.3 reduce.22
  20.0 18.8 %all-gather.7.cloned.1.call-done = bf16[8,2,1,1,128,512]{5,4,3,2,1,0:T(8,128)(2,1)} async-done(((bf16[1,2,1,1,128,512]{5,4,3,2,1,0:T(8,128)(2,1)}), bf16[8,2,1,1,128,512]{5,4,3,2,1,0:T(8,128)(2,1)}) %all-gather.7.cloned.1.call-update) | async-done | bytes 2097168 | tf_op jit(solution)/shard_map/all_gather | solution.py:38
  38.8 3.1 copy.49
  41.9 36.4 %while.11 = (s32[]{:T(128)}, bf16[8,8,128,256]{3,2,1,0:T(8,128)(2,1)}, s32[8,3,8]{2,0,1:T(8,128)S(1)}, bf16[2,128,512]{2,1,0:T(8,128)(2,1)S(1)}, bf16[2,4,2,128,...) while((s32[]{:T(128)}, bf16[8,8,128,256]{3,2,1,0:T(8,128)(2,1)}, s32[8,3,8]{2,0,1:T(8,128)S(1)}, ...), condition=%wide.region_6.7_spmd, body=%wide.region_5.6_spmd.sunk | while | flops 268959872 | bytes 9962529 | solution.py:67
  41.9 2.3 gather_fusion.1
  44.9 1.6 fusion.43
  46.5 2.3 gather_fusion.1
  49.4 1.6 fusion.43
  51.0 2.3 gather_fusion.1
  53.9 1.6 fusion.43
  55.6 2.3 gather_fusion.1
  58.5 1.6 fusion.43
  60.1 2.3 gather_fusion.1
  63.1 1.6 fusion.43
  64.7 2.3 gather_fusion.1
  67.6 1.6 fusion.43
  69.2 2.3 gather_fusion.1
  72.2 1.6 fusion.43
  73.8 2.3 gather_fusion.1
  76.7 1.6 fusion.43
  78.3 4.5 %bitcast_select_fusion = bf16[64,128,256]{2,1,0:T(8,128)(2,1)} fusion(bf16[8,8,128,256]{3,2,1,0:T(8,128)(2,1)} %get-tuple-element.32, pred[64]{0:T(512)(128)(4,1)S(1)} %and_bitcast_fusion), kind=kLoop, calls=%fused_computation.24 | loop fusion | flops 2097152 | bytes 8388672 | tf_op jit(solution)/shard_map/jit(_where)/select_n | solution.py:70
  82.8 8.6 %gather_fusion.3 = bf16[128,128,256]{2,1,0:T(8,128)(2,1)} fusion(bf16[64,128,256]{2,1,0:T(8,128)(2,1)} %bitcast_select_fusion, s32[1024]{0:T(1024)S(1)} %pad_clamp_fusion), kind=kCustom, calls=%fused_computation.3 | custom fusion | bytes 16777728 | tf_op jit(solution)/shard_map/gather | solution.py:85
  91.5 7.2 %broadcast_select_fusion = bf16[128,128,256]{2,1,0:T(8,128)(2,1)} fusion(bf16[128,128,256]{2,1,0:T(8,128)(2,1)} %gather_fusion.3, pred[128]{0:T(512)(128)(4,1)S(1)} %fusion.20), kind=kLoop, calls=%fused_computation.23 | loop fusion | flops 4194304 | bytes 16777344 | tf_op jit(solution)/shard_map/jit(_where)/select_n | solution.py:85
  98.7 6.0 %all-to-all-start.1 = ((bf16[128,128,256]{2,1,0:T(8,128)(2,1)}), bf16[128,128,256]{2,1,0:T(8,128)(2,1)}, u32[]{:S(2)}, u32[]{:S(2)}) async-start(bf16[128,128,256]{2,1,0:T(8,128)(2,1)} %broadcast_select_fusion), calls=%async_computation.1 | async-start | bytes 16777216 | tf_op jit(solution)/shard_map/all_to_all | solution.py:88
  104.7 1.9 copy.46
  107.3 177.3 %all-to-all-done.1 = bf16[128,128,256]{2,1,0:T(8,128)(2,1)} async-done(((bf16[128,128,256]{2,1,0:T(8,128)(2,1)}), bf16[128,128,256]{2,1,0:T(8,128)(2,1)}, u32[]{:S(2)}, u32[]{:S(2)}) %all-to-all-start.1) | async-done | bytes 8388640 | tf_op jit(solution)/shard_map/all_to_all | solution.py:88
  284.6 7.9 %fusion.8 = f32[2,8,128,256]{3,1,0,2:T(8,128)S(1)} fusion(bf16[128,128,256]{2,1,0:T(8,128)(2,1)} %all-to-all-done.1, s32[128]{0:T(128)S(1)} %eq.71), kind=kOutput, calls=%fused_computation.28 | convolution fusion | flops 134219776 | bytes 10486272 | tf_op jit(solution)/shard_map/sk,sij->kij/dot_general | solution.py:93
  292.5 1.9 copy.51
  294.4 2.4 bitcast_add_fusion
  296.9 2.7 all-gather.1
  300.7 42.9 %all-reduce.4.cloned.1.call-done = f32[256,256]{0,1:T(8,128)} async-done(((f32[256,256]{0,1:T(8,128)}), f32[256,256]{0,1:T(8,128)}) %all-reduce.4.cloned.1.call-update) | async-done | bytes 262160 | tf_op jit(solution)/shard_map/psum | solution.py:11
  343.6 1.1 copy.53
  344.7 1.0 fusion.12
  345.9 11.7 %cholesky.49 = f32[128,128]{1,0:T(8,128)S(1)} custom-call(f32[128,128]{1,0:T(8,128)S(1)} %cholesky.115), custom_call_target="Cholesky" | custom-call | tf_op jit(solution)/shard_map/jit(cholesky)/cholesky | solution.py:104
  357.7 9.8 %custom-call.14 = f32[1,128,128]{1,2,0:T(8,128)S(1)} custom-call(f32[1,128,128]{2,1,0:T(8,128)S(1)} %get-tuple-element.86), custom_call_target="InvertDiagBlocksLowerTriangular" | custom-call | tf_op jit(solution)/shard_map/jit(cholesky)/cholesky | solution.py:104
  368.0 11.7 %cholesky.103 = f32[128,128]{1,0:T(8,128)S(1)} custom-call(f32[128,128]{1,0:T(8,128)S(1)} %convolution_subtract_fusion.1), custom_call_target="Cholesky" | custom-call | tf_op jit(solution)/shard_map/jit(cholesky)/cholesky | solution.py:104
  381.9 4.3 while.12
  382.7 1.4 bitcast_dynamic-update-slice_fusion.2
  384.7 1.4 bitcast_dynamic-update-slice_fusion.2
  386.2 19.7 %custom-call.15 = f32[2,128,128]{1,2,0:T(8,128)S(1)} custom-call(f32[2,128,128]{2,1,0:T(8,128)S(1)} %get-tuple-element.40), custom_call_target="InvertDiagBlocksLowerTriangular" | custom-call | tf_op jit(solution)/shard_map/triangular_solve | solution.py:106
  407.8 1.1 copy.58
  408.9 27.8 %all-gather.5.cloned.1.call-done = f32[8,2,128,256]{3,2,1,0:T(8,128)} async-done(((f32[1,2,128,256]{3,2,1,0:T(8,128)}), f32[8,2,128,256]{3,2,1,0:T(8,128)}) %all-gather.5.cloned.1.call-update) | async-done | bytes 2097168 | tf_op jit(solution)/shard_map/all_gather | solution.py:110
  436.7 3.4 convolution_bitcast_fusion
  440.7 1.8 copy.59
  (79 shorter events, 15.5 us)
Async XLA Ops:
  6.5 2.1 copy-start
  6.5 32.2 %all-gather.7.cloned.1.call-start = ((), (), s32[]{:S(2)}) async-start(), calls=%async_computation.4 | async-start | bytes 2359296 | tf_op jit(solution)/shard_map/all_gather | solution.py:38
  10.6 88.0 %all-to-all-start = ((s32[4,32,1]{1,2,0:T(1,128)}), s32[4,32,1]{1,2,0:T(1,128)S(1)}, u32[]{:S(2)}, u32[]{:S(2)}) async-start(s32[4,32,1]{1,2,0:T(1,128)} %bitcast.12), calls=%async_computation | async-start | bytes 4096 | tf_op jit(solution)/shard_map/all_to_all | solution.py:89
  38.8 3.1 copy-start.2
  98.7 6.0 %copy-start.3 = (f32[1,2,1,1,128,2048]{5,4,3,2,1,0:T(8,128)S(1)}, f32[1,2,1,1,128,2048]{5,4,3,2,1,0:T(8,128)}, u32[]{:S(2)}) copy-start(f32[1,2,1,1,128,2048]{5,4,3,2,1,0:T(8,128)} %param.17) | copy-start | bytes 6291460
  98.7 186.0 %all-to-all-start.1 = ((bf16[128,128,256]{2,1,0:T(8,128)(2,1)}), bf16[128,128,256]{2,1,0:T(8,128)(2,1)}, u32[]{:S(2)}, u32[]{:S(2)}) async-start(bf16[128,128,256]{2,1,0:T(8,128)(2,1)} %broadcast_select_fusion), calls=%async_computation.1 | async-start | bytes 16777216 | tf_op jit(solution)/shard_map/all_to_all | solution.py:88
  104.7 238.9 %all-reduce.4.cloned.1.call-start = ((), (), s32[]{:S(2)}) async-start(), calls=%async_computation.2 | async-start | bytes 524288 | tf_op jit(solution)/shard_map/psum | solution.py:11
  300.3 136.4 %all-gather.5.cloned.1.call-start = ((), (), s32[]{:S(2)}) async-start(), calls=%async_computation.3 | async-start | bytes 2359296 | tf_op jit(solution)/shard_map/all_gather | solution.py:110
  440.6 2.0 copy-start.1
Sparse Core Ops, SparseCore 0:
  9.2 29.4 all-gather.6
  300.4 43.1 all-reduce.3
  407.9 28.7 all-gather.4
where the time goes:
time: 451 us; the launch traced here: 449 us
  waiting for transfers between devices  268 us (59%)
  other arithmetic  75.5 us (17%)
  local copies, waits for them, and re-layouts  50.8 us (11%)
  matrix products  25.8 us (6%)
  between operations  15.4 us (3%)
  starting transfers between devices  11 us (2%)
    all_to_all x1, waiting for transfers between devices, per_device(): lax.all_to_all(outgoing, 'front', split_axis=0, concat_axis=0, tiled=True)  177 us
    psum x1, waiting for transfers between devices, broadcast(): return lax.psum(block, axis)  42.9 us
    another operation x6, other arithmetic, per_device(): lower_factor = jnp.linalg.cholesky(pivot_block)  34 us
    all_gather x1, waiting for transfers between devices, per_device(): lax.all_gather(panel_rows.reshape(1, parent_local, half_rows, BLOCK), ('l...  27.8 us
    another operation x4, other arithmetic, per_device(): lax.linalg.triangular_solve(lower_factor, first_column, left_side=False,...  19.7 us
    all_gather x1, waiting for transfers between devices, per_device(): lax.all_gather(own_rows.reshape(1, child_local, half_rows, panel_width),...  18.8 us
    gather x8, local copies, waits for them, and re-layouts, one_tile(): panel_view[:, grid_pick, local_pick].reshape(BLOCK, panel_width)  18.2 us
    dot_general x8, matrix products, one_tile(): jnp.einsum('ik,jk->ij', left_rows, right_rows, preferred_element_type=jnp...  13 us
  transfers between devices with their start and end apart: 5, of which 4 were waited for; matrix products, arithmetic and copies ran while one was open for 16% of the time, Pallas kernels for 0%

commit v1 on v0

v1 whole, which is shorter than its diff:
```python
import functools

import jax
import jax.numpy as jnp
from jax import lax
from jax.experimental import pallas as pl
from jax.experimental.pallas import tpu as pltpu
from jax.sharding import PartitionSpec as P

BLOCK = 256
NB = 32
SUB = 8
HIGHEST = lax.Precision.HIGHEST
NT = (((1,), (1,)), ((), ()))
TN = (((0,), (0,)), ((), ()))


def eliminate(work):
    n = BLOCK
    row_ids = lax.broadcasted_iota(jnp.int32, (NB, 1), 0)
    for kb in range(n // NB):
        base = kb * NB
        lo, hi = (0, n + n // 2) if base < n // 2 else (n // 2, 2 * n)
        rows = work[base : base + NB, lo:hi]
        for sub in range(NB // SUB):
            first = base - lo + sub * SUB
            cols = [
                jnp.broadcast_to(rows[:, first + i : first + i + 1], (NB, 128))
                for i in range(SUB)
            ]
            for i in range(SUB):
                j = sub * SUB + i
                inv = lax.rsqrt(cols[i][j : j + 1, :])
                below = jnp.where(row_ids > j, cols[i] * inv, 0.0)
                for m in range(i + 1, SUB):
                    cols[m] = cols[m] - below * (cols[m][j : j + 1, :] * inv)
                width = hi - lo
                inv_wide = jnp.concatenate([inv] * (width // 128), axis=1)
                below_wide = jnp.concatenate([below] * (width // 128), axis=1)
                urow = rows[j : j + 1, :] * inv_wide
                rows = jnp.where(row_ids == j, urow, rows - below_wide * urow)
        work[base : base + NB, lo:hi] = rows
        rest = base + NB
        if rest < n:
            left = rows[:, rest // 128 * 128 - lo : n - lo]
            update = lax.dot_general(
                left, rows, TN, precision=HIGHEST, preferred_element_type=jnp.float32
            )
            work[rest:n, lo:hi] = work[rest:n, lo:hi] - update[rest - rest // 128 * 128 :, :]


def factor_tail(acc, pivot, work, panel_ref):
    n = BLOCK
    whole = pivot[...]
    work[:, :n] = 0.5 * (whole + whole.T)
    work[:, n:] = (
        lax.broadcasted_iota(jnp.int32, (n, n), 0) == lax.broadcasted_iota(jnp.int32, (n, n), 1)
    ).astype(jnp.float32)
    eliminate(work)
    local, half = acc.shape[0], acc.shape[1]
    column = acc[:, :, :n].reshape(local * half, n)
    panel = lax.dot_general(
        column, work[:, n:], NT, precision=HIGHEST, preferred_element_type=jnp.float32
    )
    panel_ref[...] = panel.reshape(local, half, n)


def assemble_kernel(
    count_ref, own_list, pivot_list, gathered, own_rows, parent, raw_pivot,
    acc, panel_ref, tiles, pivot_tiles, pivot, work,
):
    fronts, grids, levels, local, half, depth = gathered.shape
    blocks = grids * local

    def gram(step, carry):
        f, g = step // grids, step % grids
        right = gathered[f, g].reshape(levels * local * half, depth)
        left = jnp.concatenate(
            [own_rows[f].reshape(local * half, depth)]
            + [gathered[f, 0].reshape(levels * local * half, depth)],
            axis=0,
        )
        prod = lax.dot_general(left, right, NT, preferred_element_type=jnp.float32)
        prod = (-prod).astype(jnp.bfloat16)
        for r in range(local):
            for s in range(local):
                at = f * (local * blocks) + r * blocks + s * grids + g
                for m in range(levels):
                    lane = (m * local + s) * half
                    tiles[at, :, m * half : (m + 1) * half] = prod[
                        r * half : (r + 1) * half, lane : lane + half
                    ]
                    for lv in range(levels):
                        row = (local + lv * local + r) * half
                        pivot_tiles[lv, at, :, m * half : (m + 1) * half] = prod[
                            row : row + half, lane : lane + half
                        ]
        return carry

    lax.fori_loop(0, fronts * grids, gram, 0)
    pivot[...] = raw_pivot[...]
    for lv in range(levels):

        def add_pivot(k, carry, lv=lv):
            at = pivot_list[lv, k]
            rows = slice(lv * half, (lv + 1) * half)
            pivot[rows, :] = pivot[rows, :] + pivot_tiles[lv, at].astype(jnp.float32)
            return carry

        lax.fori_loop(0, count_ref[1 + lv], add_pivot, 0)
    acc[...] = parent[...]
    width_blocks = parent.shape[2] // BLOCK

    def add_own(k, carry):
        code = own_list[k]
        at, place = code // 256, code % 256
        r = place // width_blocks
        lanes = pl.ds(pl.multiple_of(place % width_blocks * BLOCK, BLOCK), BLOCK)
        acc[r, :, lanes] = acc[r, :, lanes] + tiles[at].astype(jnp.float32)
        return carry

    lax.fori_loop(0, count_ref[0], add_own, 0)
    factor_tail(acc, pivot, work, panel_ref)


def tail_kernel(parent, raw_pivot, panel_ref, work):
    factor_tail(parent, raw_pivot, work, panel_ref)


def schur_kernel(acc, panel, shared, out):
    local, half, width = acc.shape
    grids, levels = shared.shape[0], shared.shape[1]
    rows = panel[...].reshape(local * half, BLOCK)
    out[:, :, :BLOCK] = panel[...]
    for g in range(grids):
        for lv in range(levels):
            for s in range(local):
                if s == 0 and g == 0:
                    continue
                prod = lax.dot_general(
                    rows, shared[g, lv, s], NT, precision=HIGHEST,
                    preferred_element_type=jnp.float32,
                ).reshape(local, half, half)
                lane = (s * grids + g) * BLOCK + lv * half
                out[:, :, lane : lane + half] = acc[:, :, lane : lane + half] - prod


VMEM = pl.BlockSpec(memory_space=pltpu.VMEM)
SMEM = pl.BlockSpec(memory_space=pltpu.SMEM)


def compact(codes, keep):
    size = codes.shape[0]
    position = jnp.cumsum(keep.astype(jnp.int32)) - 1
    match = (position[None, :] == jnp.arange(size, dtype=jnp.int32)[:, None]) & keep[None, :]
    return jnp.sum(jnp.where(match, codes[None, :], 0), axis=1), jnp.sum(keep.astype(jnp.int32))


def owner_of(parents, parent_owner):
    ids = jnp.arange(parent_owner.shape[0], dtype=jnp.int32)
    return jnp.sum(jnp.where(parents[..., None] == ids, parent_owner, 0), axis=-1)


def gather_all(
    child_panel, child_blocks, tile_rows, tile_cols, tile_parent, tile_place, parent_owner, parent_front
):
    levels, grids, fronts = lax.axis_size("lvl"), lax.axis_size("grid"), lax.axis_size("front")
    me_l, me_g, me_f = lax.axis_index("lvl"), lax.axis_index("grid"), lax.axis_index("front")
    local, half, depth = child_panel.shape[1], child_panel.shape[4], child_panel.shape[5]
    rows_in = child_panel.reshape(1, local, half, depth)
    slots = tile_rows.shape[3]
    blocks = local * grids
    row = tile_rows.reshape(slots)
    col = tile_cols.reshape(slots)
    live = (row * grids + me_g < child_blocks[0]) & (col < child_blocks[0])
    to = jnp.where(live, owner_of(tile_parent.reshape(slots), parent_owner), -1)
    meta = jnp.stack([row, col, to, tile_place.reshape(slots)])[None]
    axes = ("front", "grid", "lvl")
    meta = lax.all_gather(meta, axes, axis=0, tiled=True)
    meta = meta.reshape(fronts, grids, levels, 4, slots)
    first = parent_front[0, :1, 0, 0, :, :BLOCK]
    raw_pivot = lax.all_gather(first, ("grid", "lvl"), axis=0, tiled=True)[:levels]
    raw_pivot = raw_pivot.reshape(levels * half, BLOCK)
    gathered = lax.all_gather(rows_in, axes, axis=0, tiled=True)
    gathered = gathered.reshape(fronts, grids, levels, local, half, depth)
    own_rows = lax.dynamic_slice(
        gathered, (0, me_g, me_l, 0, 0, 0), (fronts, 1, 1, local, half, depth)
    ).reshape(fronts, local, half, depth)
    child = jnp.arange(fronts, dtype=jnp.int32)[:, None] * (local * blocks)

    def codes_of(m):
        return child + m[:, 0] * blocks + m[:, 1]

    mine = lax.dynamic_slice(meta, (0, me_g, me_l, 0, 0), (fronts, 1, 1, 4, slots))[:, 0, 0]
    own_list, own_count = compact(
        (codes_of(mine) * 256 + mine[:, 3]).reshape(-1), (mine[:, 2] == me_f).reshape(-1)
    )
    lists, counts = [], [own_count]
    for lv in range(levels):
        m = meta[:, 0, lv]
        found, count = compact(
            codes_of(m).reshape(-1), ((m[:, 2] == me_f) & (m[:, 3] == 0)).reshape(-1)
        )
        lists.append(found)
        counts.append(count)
    parent = parent_front.reshape(parent_front.shape[1], half, parent_front.shape[5])
    return pl.pallas_call(
        assemble_kernel,
        out_shape=(
            jax.ShapeDtypeStruct(parent.shape, jnp.float32),
            jax.ShapeDtypeStruct((parent.shape[0], half, BLOCK), jnp.float32),
        ),
        in_specs=[SMEM, SMEM, SMEM, VMEM, VMEM, VMEM, VMEM],
        out_specs=(VMEM, VMEM),
        scratch_shapes=[
            pltpu.VMEM((fronts * local * blocks, half, BLOCK), jnp.bfloat16),
            pltpu.VMEM((levels, fronts * local * blocks, half, BLOCK), jnp.bfloat16),
            pltpu.VMEM((BLOCK, BLOCK), jnp.float32),
            pltpu.VMEM((BLOCK, 2 * BLOCK), jnp.float32),
        ],
        compiler_params=pltpu.CompilerParams(vmem_limit_bytes=52 * 1024 * 1024),
        name="assemble",
    )(jnp.stack(counts), own_list, jnp.stack(lists), gathered, own_rows, parent, raw_pivot)


def exchange_tiles(
    child_panel, child_blocks, tile_rows, tile_cols, tile_parent, tile_place, parent_owner, parent_front
):
    levels, grids, fronts = lax.axis_size("lvl"), lax.axis_size("grid"), lax.axis_size("front")
    grid_index = lax.axis_index("grid")
    local, half, depth = child_panel.shape[1], child_panel.shape[4], child_panel.shape[5]
    parent_local, width = parent_front.shape[1], parent_front.shape[5]
    slots = tile_rows.shape[3]
    blocks = width // BLOCK
    capacity = 2 * slots // fronts
    own = child_panel.reshape(local * half, depth)
    view = lax.all_gather(
        own.reshape(1, local, half, depth), ("grid", "lvl"), axis=0, tiled=True
    ).reshape(grids, levels, local, half, depth)
    gram = jnp.einsum("ik,glsjk->isglj", own, view, preferred_element_type=jnp.float32)
    gram = (-gram).astype(jnp.bfloat16).reshape(local, half, local * grids, BLOCK)
    gram = gram.transpose(0, 2, 1, 3).reshape(local * local * grids, half, BLOCK)
    row, col = tile_rows.reshape(slots), tile_cols.reshape(slots)
    live = (row * grids + grid_index < child_blocks[0]) & (col < child_blocks[0])
    ids = jnp.arange(fronts, dtype=jnp.int32)
    owners = owner_of(tile_parent.reshape(slots), parent_owner)
    one_hot = (owners[:, None] == ids[None, :]).astype(jnp.int32)
    rank = jnp.sum((jnp.cumsum(one_hot, axis=0) - 1) * one_hot, axis=1)
    index = owners * capacity + rank
    matches = index[None, :] == jnp.arange(fronts * capacity, dtype=jnp.int32)[:, None]
    filled = jnp.any(matches & live[None, :], axis=1)
    source = jnp.sum(jnp.where(matches, (row * local * grids + col)[None, :], 0), axis=1)
    place = jnp.sum(jnp.where(matches, tile_place.reshape(slots)[None, :], 0), axis=1)
    outgoing = jnp.where(filled[:, None, None], gram[source], jnp.zeros((), jnp.bfloat16))
    positions = jnp.where(filled, place, -1)
    incoming = lax.all_to_all(outgoing, "front", split_axis=0, concat_axis=0, tiled=True)
    landed = lax.all_to_all(positions, "front", split_axis=0, concat_axis=0, tiled=True)
    spots = parent_local * blocks
    selector = (landed[:, None] == jnp.arange(spots, dtype=jnp.int32)[None, :]).astype(jnp.bfloat16)
    contrib = jnp.einsum("sk,sij->kij", selector, incoming, preferred_element_type=jnp.float32)
    contrib = contrib.reshape(parent_local, blocks, half, BLOCK).transpose(0, 2, 1, 3)
    assembled = parent_front.reshape(parent_local, half, width) + contrib.reshape(
        parent_local, half, width
    )
    raw = lax.all_gather(assembled[0, :, :BLOCK][None], ("grid", "lvl"), axis=0, tiled=True)
    raw = raw[:levels].reshape(levels * half, BLOCK)
    panel = pl.pallas_call(
        tail_kernel,
        out_shape=jax.ShapeDtypeStruct((parent_local, half, BLOCK), jnp.float32),
        in_specs=[VMEM, VMEM],
        out_specs=VMEM,
        scratch_shapes=[pltpu.VMEM((BLOCK, 2 * BLOCK), jnp.float32)],
        name="factor",
    )(assembled, raw)
    return assembled, panel


def per_device(*args):
    levels, grids, fronts = lax.axis_size("lvl"), lax.axis_size("grid"), lax.axis_size("front")
    parent_front = args[-1]
    assembled, panel = (gather_all if fronts <= 4 else exchange_tiles)(*args)
    shared = lax.all_gather(panel[None], ("grid", "lvl"), axis=0, tiled=True)
    shared = shared.reshape((grids, levels) + panel.shape)
    result = pl.pallas_call(
        schur_kernel,
        out_shape=jax.ShapeDtypeStruct(assembled.shape, jnp.float32),
        in_specs=[VMEM, VMEM, VMEM],
        out_specs=VMEM,
        compiler_params=pltpu.CompilerParams(vmem_limit_bytes=32 * 1024 * 1024),
        name="schur",
    )(assembled, panel, shared)
    return result.reshape(parent_front.shape)


def solution(mesh):
    return jax.shard_map(
        per_device,
        mesh=mesh,
        in_specs=(
            P("front", None, "grid", "lvl", None, None),
            P("front"),
            P("lvl", "front", "grid", None),
            P("lvl", "front", "grid", None),
            P("lvl", "front", "grid", None, None),
            P("lvl", "front", "grid", None),
            P(),
            P("front", None, "grid", "lvl", None, None),
        ),
        out_specs=P("front", None, "grid", "lvl", None, None),
        check_vma=False,
    )
```

time: 451 us -> 186 us (0.41)
  waiting for transfers between devices: 268 us -> 88 us
  other arithmetic: 75.5 us -> 7.95 us
  local copies, waits for them, and re-layouts: 50.8 us -> 8.81 us
  blocking collectives: 2.68 us -> 36.2 us
  Pallas kernels: 0 us -> 29.7 us
  matrix products: 25.8 us -> 0 us
  starting transfers between devices: 11 us -> 0.08 us
    all_to_all x2 -> x0, waiting for transfers between devices: 177 us -> none  [the longest x1 177 us: per_device(): lax.all_to_all(outgoing, 'front', split_axis=0, concat_axis=0, tiled=True)]
    another operation x11 -> x8, other arithmetic: 53.9 us -> 3.06 us  [the longest x1 2.01 us: gather_all(): jnp.stack(counts)]
    psum x1 -> x0, waiting for transfers between devices: 42.9 us -> none  [broadcast(): return lax.psum(block, axis)]
    all_gather x2 -> x3, waiting for transfers between devices: 46.6 us -> 87.2 us  [the longest x1 58.2 us: gather_all(): gathered = lax.all_gather(rows_in, axes, axis=0, tiled=True)]
    all_gather x1, blocking collectives: 2.68 us -> 36.2 us  [gather_all(): meta = lax.all_gather(meta, axes, axis=0, tiled=True)]
    gather x18 -> x0, local copies, waits for them, and re-layouts: 33 us -> none  [the longest x8 18.2 us: one_tile(): panel_view[:, grid_pick, local_pick].reshape(BLOCK, panel_width)]
    pallas_call x0 -> x2, Pallas kernels: none -> 29.7 us  [the longest x1 24.4 us: gather_all(): pl.pallas_call(assemble_kernel, out_shape=(jax.ShapeDtypeStruct(parent.sh...]
    dot_general x10 -> x0, matrix products: 24.3 us -> none  [the longest x8 13 us: one_tile(): jnp.einsum('ik,jk->ij', left_rows, right_rows, preferred_element_type=jnp...]
  transfers between devices with their start and end apart: 5 -> 3, of which waited for: 4 -> 2; matrix products, arithmetic and copies ran while one was open for 16% -> 6% of each run, Pallas kernels for 0% -> 0%
where the time goes in v1:
time: 186 us; the launch traced here: 185 us
  waiting for transfers between devices  88 us (47%)
  blocking collectives  36.2 us (19%)
  Pallas kernels  29.7 us (16%)
  between operations  13.8 us (7%)
  local copies, waits for them, and re-layouts  8.81 us (5%)
  other arithmetic  7.95 us (4%)
    all_gather x1, waiting for transfers between devices, gather_all(): gathered = lax.all_gather(rows_in, axes, axis=0, tiled=True)  58.2 us
    all_gather x1, blocking collectives, gather_all(): meta = lax.all_gather(meta, axes, axis=0, tiled=True)  36.2 us
    all_gather x1, waiting for transfers between devices, per_device(): shared = lax.all_gather(panel[None], ('grid', 'lvl'), axis=0, tiled=True)  29 us
    pallas_call x1, Pallas kernels, gather_all(): pl.pallas_call(assemble_kernel, out_shape=(jax.ShapeDtypeStruct(parent.sh...  24.4 us
    pallas_call x1, Pallas kernels, per_device(): pl.pallas_call(schur_kernel, out_shape=jax.ShapeDtypeStruct(assembled.sha...  5.31 us
  transfers between devices with their start and end apart: 3, of which 2 were waited for; matrix products, arithmetic and copies ran while one was open for 6% of the time, Pallas kernels for 0%

profile of v1, /device:TPU:9, one launch (start us, length us, event | category | flops | bytes accessed | tf_op | source)
XLA Modules:
  0.0 184.6 jit_solution(2145025307739440266)
XLA Ops:
  6.5 1.6 slice.89
  8.2 0.7 all-gather.9.cloned.1.call-update
  9.6 0.1 add.113
  9.7 0.1 add.114
  9.7 0.8 select_reduce_fusion.3
  10.5 0.7 and_select_fusion
  11.2 0.7 add_bitcast_fusion
  11.9 36.2 %all-gather.4 = s32[32,4,64]{2,1,0:T(4,128)S(1)} all-gather(s32[1,4,64]{2,1,0:T(4,128)S(1)} %add_bitcast_fusion), channel_id=2, replica_groups=mesh['lvl'=2,'front'=4,'grid'=4] {'front','grid','lvl'}, dimensions={0}, use_global_device_ids=true | all-gather | bytes 33792 | tf_op jit(solution)/shard_map/all_gather | solution.py:179
  48.2 0.1 reshape.289
  48.2 0.3 reduce-window.25
  48.5 0.1 mul.69
  48.6 0.1 eq.134
  48.7 0.1 squeeze.41
  48.8 0.1 squeeze.40
  48.9 0.1 slice.76
  49.0 0.1 reshape.291
  49.1 0.3 reduce-window.37
  49.4 0.1 mul.75
  49.5 0.1 and.73
  49.6 0.1 squeeze.43
  49.6 0.1 slice.85
  49.8 0.1 reshape.290
  49.8 0.3 reduce-window.29
  50.2 0.1 mul.73
  50.2 0.1 and.70
  50.3 0.1 squeeze.42
  50.4 0.1 slice.81
  50.5 0.7 convert_reduce_fusion.2
  51.2 0.7 convert_reduce_fusion
  51.9 0.7 convert_reduce_fusion.1
  52.6 2.0 %pad_add_fusion.1.count_ref = s32[3]{0:T(128)S(1)} fusion(s32[1]{0:T(128)} %bitcast.13, s32[1]{0:T(128)} %bitcast.11, s32[1]{0:T(128)} %bitcast.9), kind=kLoop, calls=%fused_computation.40 | loop fusion | flops 6 | bytes 24 | tf_op jit(solution)/shard_map/stack | solution.py:223
  54.6 0.1 slice_reduce_fusion
  54.7 0.1 slice_reduce_fusion.1
  54.8 0.1 add_bitcast_fusion.1
  54.9 0.1 select_reduce_fusion
  55.1 0.1 add_bitcast_fusion.2
  55.1 0.1 select_reduce_fusion.1
  55.3 0.1 slice_reduce_fusion.2
  55.4 0.1 add_bitcast_fusion.3
  55.5 0.1 select_reduce_fusion.2.own_list
  55.7 1.0 slice.106
  56.6 58.2 %all-gather.9.cloned.1.call-done = bf16[32,2,1,1,128,512]{5,4,3,2,1,0:T(8,128)(2,1)} async-done(((bf16[1,2,1,1,128,512]{5,4,3,2,1,0:T(8,128)(2,1)}), bf16[32,2,1,1,128,512]{5,4,3,2,1,0:T(8,128)(2,1)}) %all-gather.9.cloned.1.call-update) | async-done | bytes 8388624 | tf_op jit(solution)/shard_map/all_gather | solution.py:184
  114.8 1.3 dynamic-slice_bitcast_fusion.own_rows
  116.1 24.4 %assemble.1 = (f32[2,128,2048]{2,1,0:T(8,128)}, f32[2,128,256]{2,1,0:T(8,128)}) custom-call(s32[3]{0:T(128)S(1)} %pad_add_fusion.1.count_ref, s32[256]{0:T(256)S(1)} %select_reduce_fusion.2.own_list, s32[2,256]{1,0:T(2,128)S(1)} %pad_add_fusion.pivot_list, bf16[4,4,2,2,128,512]{5,4,3,2,1,0:T(8,128)(2,1)} %bitcast.69, ...), custom_call_target="tpu_custom_call" | custom-call | tf_op jit(solution)/shard_map/assemble/pallas_call | solution.py:207
  140.6 29.0 %all-gather.13.cloned.1.call-done = f32[16,128,256]{2,1,0:T(8,128)} async-done(((f32[2,128,256]{2,1,0:T(8,128)}), f32[16,128,256]{2,1,0:T(8,128)}) %all-gather.13.cloned.1.call-update) | async-done | bytes 2097168 | tf_op jit(solution)/shard_map/all_gather | solution.py:282
  169.6 1.6 copy-done
  171.2 1.6 copy-done.1
  172.8 5.3 %schur.1 = f32[2,128,2048]{2,1,0:T(8,128)} custom-call(f32[2,128,2048]{2,1,0:T(8,128)S(1)} %copy-done, f32[2,128,256]{2,1,0:T(8,128)} %get-tuple-element.8.panel, f32[4,2,2,128,256]{4,3,2,1,0:T(8,128)S(1)} %bitcast.66), custom_call_target="tpu_custom_call" | custom-call | tf_op jit(solution)/shard_map/schur/pallas_call | solution.py:284
  (23 shorter events, 0.3 us)
Async XLA Ops:
  6.5 49.1 %all-gather.11.cloned.1.call-start = ((), (), s32[]{:S(2)}) async-start(), calls=%async_computation.1 | async-start | bytes 1179648 | tf_op jit(solution)/shard_map/all_gather | solution.py:182
  8.1 106.7 %all-gather.9.cloned.1.call-start = ((), (), s32[]{:S(2)}) async-start(), calls=%async_computation | async-start | bytes 8650752 | tf_op jit(solution)/shard_map/all_gather | solution.py:184
  8.9 160.7 %all-gather.13.cloned.1.call-start = ((), (), s32[]{:S(2)}) async-start(), calls=%async_computation.2 | async-start | bytes 2359296 | tf_op jit(solution)/shard_map/all_gather | solution.py:282
  169.6 1.6 copy-start
  171.2 1.6 copy-start.1
Sparse Core Ops, SparseCore 0:
  9.2 25.1 all-gather.10
  37.3 77.4 all-gather.8
  140.7 28.8 all-gather.12

commit v2 on v1

--- a/solution.py
+++ b/solution.py
@@ -145,7 +145,195 @@
                 out[:, :, lane : lane + half] = acc[:, :, lane : lane + half] - prod
 
 
+class Sends:
+    def __init__(self, send_sems, recv_sems):
+        self.send_sems, self.recv_sems, self.used, self.started = send_sems, recv_sems, 0, []
+
+    def make(self, src, dst, device):
+        copy = pltpu.make_async_remote_copy(
+            src_ref=src,
+            dst_ref=dst,
+            send_sem=self.send_sems.at[self.used],
+            recv_sem=self.recv_sems.at[self.used],
+            device_id=device,
+            device_id_type=pl.DeviceIdType.MESH,
+        )
+        self.used += 1
+        return copy
+
+    def start(self, src, dst, device):
+        copy = self.make(src, dst, device)
+        copy.start()
+        self.started.append(copy)
+        return copy
+
+    def finish(self):
+        for copy in self.started:
+            copy.wait_send()
+
+
+def greet(devices):
+    barrier = pltpu.get_barrier_semaphore()
+    for device in devices:
+        pl.semaphore_signal(barrier, inc=1, device_id=device, device_id_type=pl.DeviceIdType.MESH)
+    pl.semaphore_wait(barrier, len(devices))
+
+
+def plane_peers():
+    level, grid = lax.axis_index("lvl"), lax.axis_index("grid")
+    across = grid + 1 - 2 * (grid % 2)
+    along = (grid + 2) % 4
+    return level, grid, across, along
+
+
+def gather_kernel(
+    own, meta, first, out, meta_own, meta_pivot, raw, send_sems, recv_sems, local_sems
+):
+    level, grid, across, along = plane_peers()
+    corner = (across + 2) % 4
+    front = lax.axis_index("front")
+    order = [front + 1 - 2 * (front % 2), (front + 2) % 4, 3 - front]
+
+    def at_front(f):
+        return {"front": f}
+
+    x_peer, y_peer, core = {"grid": across}, {"grid": along}, {"lvl": 1 - level}
+    greet([at_front(f) for f in order] + [x_peer, y_peer, {"grid": corner}, core])
+    sends = Sends(send_sems, recv_sems)
+    locals_ = [
+        pltpu.make_async_copy(own, out.at[front, grid, level], local_sems.at[0]),
+        pltpu.make_async_copy(meta, meta_own.at[front], local_sems.at[1]),
+    ]
+    for copy in locals_:
+        copy.start()
+    meta_z = [sends.start(meta, meta_own.at[front], at_front(f)) for f in order]
+    panel_z = [sends.start(own, out.at[front, grid, level], at_front(f)) for f in order]
+    to_x, to_y, to_core = [], [], []
+
+    def spread(f, source):
+        place = out.at[f, grid, level]
+        to_x.append(sends.start(source, place, x_peer))
+        to_y.append(sends.start(source, place, y_peer))
+        to_core.append(sends.start(source, place, core))
+
+    spread(front, own)
+    planes = [front] + order
+
+    raw_at = raw.at[level]
+    piv_at = meta_pivot.at[level]
+    raw_copies = [sends.make(first, raw_at, {"grid": g}) for g in (1, 2, 3)]
+    piv_copies = [sends.make(meta_own, piv_at, {"grid": g}) for g in (1, 2, 3)]
+    raw_local = pltpu.make_async_copy(first, raw_at, local_sems.at[2])
+    piv_local = pltpu.make_async_copy(meta_own, piv_at, local_sems.at[3])
+
+    locals_[1].wait()
+    for copy in meta_z:
+        copy.wait_recv()
+
+    @pl.when(grid == 0)
+    def _():
+        piv_local.start()
+        raw_local.start()
+        for copy in piv_copies + raw_copies:
+            copy.start()
+        piv_local.wait()
+        raw_local.wait()
+
+    for g in (1, 2, 3):
+
+        @pl.when(grid == g)
+        def _(g=g):
+            piv_copies[g - 1].wait_recv()
+            raw_copies[g - 1].wait_recv()
+
+    small = [sends.start(piv_at, piv_at, core), sends.start(raw_at, raw_at, core)]
+    corners = []
+
+    def forward(k):
+        f = planes[k]
+        to_x[k].wait_recv()
+        place = out.at[f, across, level]
+        half = out.at[f, across, level, 0]
+        corners.append(sends.start(half, half, y_peer))
+        to_core.append(sends.start(place, place, core))
+        to_y[k].wait_recv()
+        place = out.at[f, along, level]
+        half = out.at[f, along, level, 1]
+        corners.append(sends.start(half, half, x_peer))
+        to_core.append(sends.start(place, place, core))
+
+    def corner_in(k):
+        place = out.at[planes[k], corner, level]
+        corners[2 * k].wait_recv()
+        corners[2 * k + 1].wait_recv()
+        to_core.append(sends.start(place, place, core))
+
+    for k in (1, 2, 3):
+        panel_z[k - 1].wait_recv()
+        place = out.at[planes[k], grid, level]
+        spread(planes[k], place)
+        forward(k - 1)
+        if k > 1:
+            corner_in(k - 2)
+    forward(3)
+    corner_in(2)
+    corner_in(3)
+    locals_[0].wait()
+    for copy in to_core + small:
+        copy.wait_recv()
+    sends.finish()
+
+    @pl.when(grid == 0)
+    def _():
+        for copy in piv_copies + raw_copies:
+            copy.wait_send()
+
+
+def share_kernel(own, out, send_sems, recv_sems, local_sem):
+    level, grid, across, along = plane_peers()
+    corner = (across + 2) % 4
+    x_peer, y_peer, core = {"grid": across}, {"grid": along}, {"lvl": 1 - level}
+    greet([x_peer, y_peer, core])
+    sends = Sends(send_sems, recv_sems)
+    local = out.shape[2]
+    mine = pltpu.make_async_copy(own, out.at[grid, level], local_sem)
+    to_x = [None] * local
+    to_y = [None] * local
+    to_core = []
+    for r in range(local):
+        place = out.at[grid, level, r]
+        to_x[r] = sends.start(own.at[r], place, x_peer)
+        place = out.at[grid, level, local - 1 - r]
+        to_y[local - 1 - r] = sends.start(own.at[local - 1 - r], place, y_peer)
+    to_core.append(sends.start(own, out.at[grid, level], core))
+    mine.start()
+    to_x[0].wait_recv()
+    half = out.at[across, level, 0]
+    corner_y = sends.start(half, half, y_peer)
+    to_y[1].wait_recv()
+    half = out.at[along, level, 1]
+    corner_x = sends.start(half, half, x_peer)
+    for r in range(1, local):
+        to_x[r].wait_recv()
+    place = out.at[across, level]
+    to_core.append(sends.start(place, place, core))
+    to_y[0].wait_recv()
+    place = out.at[along, level]
+    to_core.append(sends.start(place, place, core))
+    corner_y.wait_recv()
+    half = out.at[corner, level, 0]
+    to_core.append(sends.start(half, half, core))
+    corner_x.wait_recv()
+    half = out.at[corner, level, 1]
+    to_core.append(sends.start(half, half, core))
+    mine.wait()
+    for copy in to_core:
+        copy.wait_recv()
+    sends.finish()
+
+
 VMEM = pl.BlockSpec(memory_space=pltpu.VMEM)
+ANY = pl.BlockSpec(memory_space=pl.ANY)
 SMEM = pl.BlockSpec(memory_space=pltpu.SMEM)
 
 
@@ -174,15 +362,28 @@
     col = tile_cols.reshape(slots)
     live = (row * grids + me_g < child_blocks[0]) & (col < child_blocks[0])
     to = jnp.where(live, owner_of(tile_parent.reshape(slots), parent_owner), -1)
-    meta = jnp.stack([row, col, to, tile_place.reshape(slots)])[None]
-    axes = ("front", "grid", "lvl")
-    meta = lax.all_gather(meta, axes, axis=0, tiled=True)
-    meta = meta.reshape(fronts, grids, levels, 4, slots)
-    first = parent_front[0, :1, 0, 0, :, :BLOCK]
-    raw_pivot = lax.all_gather(first, ("grid", "lvl"), axis=0, tiled=True)[:levels]
+    meta = jnp.stack([row, col, to, tile_place.reshape(slots)])
+    gathered, meta_own, meta_pivot, raw_pivot = pl.pallas_call(
+        gather_kernel,
+        out_shape=(
+            jax.ShapeDtypeStruct((fronts, grids, levels, local, half, depth), jnp.bfloat16),
+            jax.ShapeDtypeStruct((fronts, 4, slots), jnp.int32),
+            jax.ShapeDtypeStruct((levels, fronts, 4, slots), jnp.int32),
+            jax.ShapeDtypeStruct((levels, half, BLOCK), jnp.float32),
+        ),
+        in_specs=[VMEM, VMEM, VMEM],
+        out_specs=(VMEM, VMEM, VMEM, VMEM),
+        scratch_shapes=[
+            pltpu.SemaphoreType.DMA((64,)),
+            pltpu.SemaphoreType.DMA((64,)),
+            pltpu.SemaphoreType.DMA((4,)),
+        ],
+        compiler_params=pltpu.CompilerParams(
+            collective_id=0, has_side_effects=True, vmem_limit_bytes=24 * 1024 * 1024
+        ),
+        name="gather",
+    )(rows_in[0], meta, parent_front[0, 0, 0, 0, :, :BLOCK])
     raw_pivot = raw_pivot.reshape(levels * half, BLOCK)
-    gathered = lax.all_gather(rows_in, axes, axis=0, tiled=True)
-    gathered = gathered.reshape(fronts, grids, levels, local, half, depth)
     own_rows = lax.dynamic_slice(
         gathered, (0, me_g, me_l, 0, 0, 0), (fronts, 1, 1, local, half, depth)
     ).reshape(fronts, local, half, depth)
@@ -191,13 +392,13 @@
     def codes_of(m):
         return child + m[:, 0] * blocks + m[:, 1]
 
-    mine = lax.dynamic_slice(meta, (0, me_g, me_l, 0, 0), (fronts, 1, 1, 4, slots))[:, 0, 0]
+    mine = meta_own
     own_list, own_count = compact(
         (codes_of(mine) * 256 + mine[:, 3]).reshape(-1), (mine[:, 2] == me_f).reshape(-1)
     )
     lists, counts = [], [own_count]
     for lv in range(levels):
-        m = meta[:, 0, lv]
+        m = meta_pivot[lv]
         found, count = compact(
             codes_of(m).reshape(-1), ((m[:, 2] == me_f) & (m[:, 3] == 0)).reshape(-1)
         )
@@ -278,9 +479,20 @@
 def per_device(*args):
     levels, grids, fronts = lax.axis_size("lvl"), lax.axis_size("grid"), lax.axis_size("front")
     parent_front = args[-1]
-    assembled, panel = (gather_all if fronts <= 4 else exchange_tiles)(*args)
-    shared = lax.all_gather(panel[None], ("grid", "lvl"), axis=0, tiled=True)
-    shared = shared.reshape((grids, levels) + panel.shape)
+    assembled, panel = (gather_all if fronts == 4 else exchange_tiles)(*args)
+    shared = pl.pallas_call(
+        share_kernel,
+        out_shape=jax.ShapeDtypeStruct((grids, levels) + panel.shape, jnp.float32),
+        in_specs=[VMEM],
+        out_specs=VMEM,
+        scratch_shapes=[
+            pltpu.SemaphoreType.DMA((12,)),
+            pltpu.SemaphoreType.DMA((12,)),
+            pltpu.SemaphoreType.DMA,
+        ],
+        compiler_params=pltpu.CompilerParams(collective_id=1, has_side_effects=True),
+        name="share",
+    )(panel)
     result = pl.pallas_call(
         schur_kernel,
         out_shape=jax.ShapeDtypeStruct(assembled.shape, jnp.float32),

time: 186 us -> 114 us (0.61)
  waiting for transfers between devices: 88 us -> 0 us
  Pallas kernels: 29.7 us -> 95.1 us
  blocking collectives: 36.2 us -> 0 us
  between operations: 13.8 us -> 0.77 us
    all_gather x3 -> x0, waiting for transfers between devices: 87.2 us -> none  [the longest x1 58.2 us: gather_all(): gathered = lax.all_gather(rows_in, axes, axis=0, tiled=True)]
    pallas_call x0 -> x2, Pallas kernels: none -> 64.4 us  [the longest x1 49.1 us: gather_all(): pl.pallas_call(gather_kernel, out_shape=(jax.ShapeDtypeStruct((fronts, gr...]
    all_gather x1 -> x0, blocking collectives: 36.2 us -> none  [gather_all(): meta = lax.all_gather(meta, axes, axis=0, tiled=True)]
    unnamed x4 -> x12, local copies, waits for them, and re-layouts: 3.18 us -> 6.47 us
    slice x3 -> x1, local copies, waits for them, and re-layouts: 2.61 us -> 0.07 us  [the longest x1 1.57 us: gather_all(): first = parent_front[0, :1, 0, 0, :, :BLOCK]]
    reduce_sum x3 -> x0, other arithmetic: 2.08 us -> none  [compact(): jnp.sum(keep.astype(jnp.int32))]
    pallas_call x1, Pallas kernels: 24.4 us -> 26.4 us  [gather_all(): pl.pallas_call(assemble_kernel, out_shape=(jax.ShapeDtypeStruct(parent.sh...]
  transfers between devices with their start and end apart: 3 -> 0, of which waited for: 2 -> 0; matrix products, arithmetic and copies ran while one was open for 6% -> 0% of each run, Pallas kernels for 0% -> 0%
where the time goes in v2:
time: 114 us
  Pallas kernels  95.1 us (83%)
  local copies, waits for them, and re-layouts  10.5 us (9%)
  other arithmetic  7.15 us (6%)
    pallas_call x1, Pallas kernels, gather_all(): pl.pallas_call(gather_kernel, out_shape=(jax.ShapeDtypeStruct((fronts, gr...  49.1 us
    pallas_call x1, Pallas kernels, gather_all(): pl.pallas_call(assemble_kernel, out_shape=(jax.ShapeDtypeStruct(parent.sh...  26.4 us
    pallas_call x1, Pallas kernels, per_device(): pl.pallas_call(share_kernel, out_shape=jax.ShapeDtypeStruct((grids, level...  15.2 us
    unnamed x12, local copies, waits for them, and re-layouts  6.47 us
    pallas_call x1, Pallas kernels, per_device(): pl.pallas_call(schur_kernel, out_shape=jax.ShapeDtypeStruct(assembled.sha...  4.35 us

profile of v2, /device:TPU:9, one launch (start us, length us, event | category | flops | bytes accessed | tf_op | source)
XLA Modules:
  0.0 113.6 jit_solution(11513649114543520585)
XLA Ops:
  0.7 0.8 select_reduce_fusion.3
  1.4 0.7 and_select_fusion
  2.1 0.1 add.109
  2.2 0.1 add.110
  2.2 0.7 pad_add_fusion.meta
  2.9 0.9 slice_bitcast_fusion.first
  3.9 0.0 copy-start.5
  3.9 0.9 copy-done.5
  4.8 49.1 %gather.1 = (bf16[4,4,2,2,128,512]{5,4,3,2,1,0:T(8,128)(2,1)S(1)}, s32[4,4,64]{2,1,0:T(4,128)S(1)}, s32[2,4,4,64]{3,2,1,0:T(4,128)S(1)}, f32[2,128,256]{2,1,0:T(8,128)S(1)}) custom-call(bf16[2,128,512]{2,1,0:T(8,128)(2,1)S(1)} %bitcast.35, s32[4,64]{1,0:T(4,128)S(1)} %pad_add_fusion.meta, f32[128,256]{1,0:T(8,128)S(1)} %slice_bitcast_fusion.first), custom_call_target="tpu_custom_call" | custom-call | tf_op jit(solution)/shard_map/gather/pallas_call | solution.py:366
  53.9 0.0 copy-start
  54.0 3.2 %copy-done = bf16[4,4,2,2,128,512]{5,4,3,2,1,0:T(8,128)(2,1)} copy-done((bf16[4,4,2,2,128,512]{5,4,3,2,1,0:T(8,128)(2,1)}, bf16[4,4,2,2,128,512]{5,4,3,2,1,0:T(8,128)(2,1)S(1)}, u32[]{:S(2)}) %copy-start) | copy-done | bytes 8388632
  57.2 0.1 eq.134
  57.3 0.6 fusion.5
  57.9 0.1 reshape.273
  58.0 0.3 reduce-window.25
  58.3 0.1 slice.74
  58.4 0.1 slice_reduce_fusion.6
  58.5 0.1 add_bitcast_fusion.2
  58.6 0.1 squeeze.38
  58.7 0.1 squeeze.37
  58.8 0.1 mul.69
  58.9 0.1 and.70
  59.0 0.1 and.73
  59.1 0.1 mul.75
  59.2 0.1 squeeze.40
  59.3 0.1 squeeze.39
  59.4 0.1 mul.73
  59.5 0.1 select_reduce_fusion.2.own_list
  59.6 0.6 convert_reduce_fusion
  60.3 1.9 %pad_add_fusion.2.count_ref = s32[3]{0:T(128)S(1)} fusion(s32[1]{0:T(128)} %bitcast.12, s32[1]{0:T(128)} %bitcast.10, s32[1]{0:T(128)} %bitcast.8), kind=kLoop, calls=%fused_computation.46 | loop fusion | flops 6 | bytes 24 | tf_op jit(solution)/shard_map/stack | solution.py:424
  62.2 0.1 reshape.275
  62.3 0.3 reduce-window.37
  62.6 0.1 slice.83
  62.7 0.1 slice_reduce_fusion.4
  62.8 0.1 add_bitcast_fusion
  62.9 0.1 select_reduce_fusion
  63.0 0.1 reshape.274
  63.1 0.3 reduce-window.29
  63.4 0.1 slice.79
  63.5 0.1 slice_reduce_fusion.5
  63.6 0.1 add_bitcast_fusion.1
  63.7 0.1 select_reduce_fusion.1
  63.9 1.3 %dynamic-slice_bitcast_fusion.own_rows = bf16[4,2,128,512]{3,2,1,0:T(8,128)(2,1)S(1)} fusion(bf16[4,4,2,2,128,512]{5,4,3,2,1,0:T(8,128)(2,1)} %copy-done, s32[]{:T(128)S(6)} %select_n.36, s32[]{:T(128)S(6)} %select_n.37), kind=kLoop, calls=%fused_computation | loop fusion | bytes 2097160 | tf_op jit(solution)/shard_map/reshape | solution.py:389
  65.2 26.4 %assemble.1 = (f32[2,128,2048]{2,1,0:T(8,128)}, f32[2,128,256]{2,1,0:T(8,128)S(1)}) custom-call(s32[3]{0:T(128)S(1)} %pad_add_fusion.2.count_ref, s32[256]{0:T(256)S(1)} %select_reduce_fusion.2.own_list, s32[2,256]{1,0:T(2,128)S(1)} %pad_add_fusion.1.pivot_list, bf16[4,4,2,2,128,512]{5,4,3,2,1,0:T(8,128)(2,1)} %copy-done, ...), custom_call_target="tpu_custom_call" | custom-call | tf_op jit(solution)/shard_map/assemble/pallas_call | solution.py:408
  91.6 0.7 copy-done.3
  92.3 15.2 %share.1.shared = f32[4,2,2,128,256]{4,3,2,1,0:T(8,128)} custom-call(f32[2,128,256]{2,1,0:T(8,128)} %copy-done.3), custom_call_target="tpu_custom_call" | custom-call | tf_op jit(solution)/shard_map/share/pallas_call | solution.py:483
  107.6 1.6 %copy-done.1 = f32[4,2,2,128,256]{4,3,2,1,0:T(8,128)S(1)} copy-done((f32[4,2,2,128,256]{4,3,2,1,0:T(8,128)S(1)}, f32[4,2,2,128,256]{4,3,2,1,0:T(8,128)}, u32[]{:S(2)}) %copy-start.1) | copy-done | bytes 2097176
  109.2 4.3 %schur.1 = f32[2,128,2048]{2,1,0:T(8,128)} custom-call(f32[2,128,2048]{2,1,0:T(8,128)S(1)} %copy-done.2, f32[2,128,256]{2,1,0:T(8,128)S(1)} %copy-done.4, f32[4,2,2,128,256]{4,3,2,1,0:T(8,128)S(1)} %copy-done.1), custom_call_target="tpu_custom_call" | custom-call | tf_op jit(solution)/shard_map/schur/pallas_call | solution.py:496
  (17 shorter events, 0.3 us)
Async XLA Ops:
  3.9 1.0 copy-start.5
  53.9 3.2 %copy-start = (bf16[4,4,2,2,128,512]{5,4,3,2,1,0:T(8,128)(2,1)}, bf16[4,4,2,2,128,512]{5,4,3,2,1,0:T(8,128)(2,1)S(1)}, u32[]{:S(2)}) copy-start(bf16[4,4,2,2,128,512]{5,4,3,2,1,0:T(8,128)(2,1)S(1)} %get-tuple-element.13.gathered) | copy-start | bytes 25165828
  91.6 0.7 copy-start.3
  92.3 15.3 %copy-start.2 = (f32[2,128,2048]{2,1,0:T(8,128)S(1)}, f32[2,128,2048]{2,1,0:T(8,128)}, u32[]{:S(2)}) copy-start(f32[2,128,2048]{2,1,0:T(8,128)} %get-tuple-element.15.acc) | copy-start | bytes 6291460
  92.3 15.3 %copy-start.4 = (f32[2,128,256]{2,1,0:T(8,128)S(1)}, f32[2,128,256]{2,1,0:T(8,128)}, u32[]{:S(2)}) copy-start(f32[2,128,256]{2,1,0:T(8,128)} %copy-done.3) | copy-start | bytes 786436
  107.6 1.6 %copy-start.1 = (f32[4,2,2,128,256]{4,3,2,1,0:T(8,128)S(1)}, f32[4,2,2,128,256]{4,3,2,1,0:T(8,128)}, u32[]{:S(2)}) copy-start(f32[4,2,2,128,256]{4,3,2,1,0:T(8,128)} %share.1.shared) | copy-start | bytes 6291460

commit v3 on v2

--- a/solution.py
+++ b/solution.py
@@ -15,69 +15,56 @@
 TN = (((0,), (0,)), ((), ()))
 
 
-def eliminate(work):
+def eliminate(work, inverse):
     n = BLOCK
     row_ids = lax.broadcasted_iota(jnp.int32, (NB, 1), 0)
-    for kb in range(n // NB):
-        base = kb * NB
-        lo, hi = (0, n + n // 2) if base < n // 2 else (n // 2, 2 * n)
-        rows = work[base : base + NB, lo:hi]
+
+    def step(kb, carry):
+        rows = work[:NB, :]
         for sub in range(NB // SUB):
-            first = base - lo + sub * SUB
+            first = sub * SUB
             cols = [
                 jnp.broadcast_to(rows[:, first + i : first + i + 1], (NB, 128))
                 for i in range(SUB)
             ]
             for i in range(SUB):
-                j = sub * SUB + i
+                j = first + i
                 inv = lax.rsqrt(cols[i][j : j + 1, :])
                 below = jnp.where(row_ids > j, cols[i] * inv, 0.0)
                 for m in range(i + 1, SUB):
                     cols[m] = cols[m] - below * (cols[m][j : j + 1, :] * inv)
-                width = hi - lo
-                inv_wide = jnp.concatenate([inv] * (width // 128), axis=1)
-                below_wide = jnp.concatenate([below] * (width // 128), axis=1)
+                inv_wide = jnp.concatenate([inv] * (2 * n // 128), axis=1)
+                below_wide = jnp.concatenate([below] * (2 * n // 128), axis=1)
                 urow = rows[j : j + 1, :] * inv_wide
                 rows = jnp.where(row_ids == j, urow, rows - below_wide * urow)
-        work[base : base + NB, lo:hi] = rows
-        rest = base + NB
-        if rest < n:
-            left = rows[:, rest // 128 * 128 - lo : n - lo]
-            update = lax.dot_general(
-                left, rows, TN, precision=HIGHEST, preferred_element_type=jnp.float32
-            )
-            work[rest:n, lo:hi] = work[rest:n, lo:hi] - update[rest - rest // 128 * 128 :, :]
-
-
-def factor_tail(acc, pivot, work, panel_ref):
-    n = BLOCK
-    whole = pivot[...]
-    work[:, :n] = 0.5 * (whole + whole.T)
-    work[:, n:] = (
-        lax.broadcasted_iota(jnp.int32, (n, n), 0) == lax.broadcasted_iota(jnp.int32, (n, n), 1)
-    ).astype(jnp.float32)
-    eliminate(work)
-    local, half = acc.shape[0], acc.shape[1]
-    column = acc[:, :, :n].reshape(local * half, n)
-    panel = lax.dot_general(
-        column, work[:, n:], NT, precision=HIGHEST, preferred_element_type=jnp.float32
-    )
-    panel_ref[...] = panel.reshape(local, half, n)
+        at = pl.ds(pl.multiple_of(kb * NB, NB), NB)
+        inverse[at, :] = pltpu.roll(rows, kb * NB + n, 1)[:, :n]
+        update = lax.dot_general(
+            rows[:, :n], rows, TN, precision=HIGHEST, preferred_element_type=jnp.float32
+        )
+        rest = work[NB:, :] - update[NB:, :]
+        work[: n - NB, :] = pltpu.roll(rest, 2 * n - NB, 1)
+        return carry
+
+    lax.fori_loop(0, n // NB, step, 0)
 
 
 def assemble_kernel(
-    count_ref, own_list, pivot_list, gathered, own_rows, parent, raw_pivot,
-    acc, panel_ref, tiles, pivot_tiles, pivot, work,
+    meta_own, meta_pivot, gathered, parent, raw_pivot, acc, pivot, tiles, pivot_tiles
 ):
     fronts, grids, levels, local, half, depth = gathered.shape
     blocks = grids * local
+    me_g, me_l = lax.axis_index("grid"), lax.axis_index("lvl")
+    most = meta_own.shape[2]
 
     def gram(step, carry):
         f, g = step // grids, step % grids
         right = gathered[f, g].reshape(levels * local * half, depth)
         left = jnp.concatenate(
-            [own_rows[f].reshape(local * half, depth)]
-            + [gathered[f, 0].reshape(levels * local * half, depth)],
+            [
+                gathered[f, me_g, me_l].reshape(local * half, depth),
+                gathered[f, 0].reshape(levels * local * half, depth),
+            ],
             axis=0,
         )
         prod = lax.dot_general(left, right, NT, preferred_element_type=jnp.float32)
@@ -98,51 +85,61 @@
         return carry
 
     lax.fori_loop(0, fronts * grids, gram, 0)
-    pivot[...] = raw_pivot[...]
+    whole = [raw_pivot[lv] for lv in range(levels)]
     for lv in range(levels):
-
-        def add_pivot(k, carry, lv=lv):
-            at = pivot_list[lv, k]
-            rows = slice(lv * half, (lv + 1) * half)
-            pivot[rows, :] = pivot[rows, :] + pivot_tiles[lv, at].astype(jnp.float32)
-            return carry
-
-        lax.fori_loop(0, count_ref[1 + lv], add_pivot, 0)
+        rows = slice(lv * half, (lv + 1) * half)
+        pivot[rows, :] = whole[lv]
+        for f in range(fronts):
+
+            def add_pivot(k, carry, lv=lv, f=f, rows=rows):
+                @pl.when(meta_pivot[lv, f, 2, k] == 0)
+                def _():
+                    at = (f * local + meta_pivot[lv, f, 0, k]) * blocks + meta_pivot[lv, f, 1, k]
+                    pivot[rows, :] = pivot[rows, :] + pivot_tiles[lv, at].astype(jnp.float32)
+
+                return carry
+
+            lax.fori_loop(0, meta_pivot[lv, f, 3, 0], add_pivot, 0)
     acc[...] = parent[...]
     width_blocks = parent.shape[2] // BLOCK
-
-    def add_own(k, carry):
-        code = own_list[k]
-        at, place = code // 256, code % 256
-        r = place // width_blocks
-        lanes = pl.ds(pl.multiple_of(place % width_blocks * BLOCK, BLOCK), BLOCK)
-        acc[r, :, lanes] = acc[r, :, lanes] + tiles[at].astype(jnp.float32)
-        return carry
-
-    lax.fori_loop(0, count_ref[0], add_own, 0)
-    factor_tail(acc, pivot, work, panel_ref)
-
-
-def tail_kernel(parent, raw_pivot, panel_ref, work):
-    factor_tail(parent, raw_pivot, work, panel_ref)
-
-
-def schur_kernel(acc, panel, shared, out):
+    for f in range(fronts):
+
+        def add_own(k, carry, f=f):
+            at = (f * local + meta_own[f, 0, k]) * blocks + meta_own[f, 1, k]
+            place = meta_own[f, 2, k]
+            r = place // width_blocks
+            lanes = pl.ds(pl.multiple_of(place % width_blocks * BLOCK, BLOCK), BLOCK)
+            acc[r, :, lanes] = acc[r, :, lanes] + tiles[at].astype(jnp.float32)
+            return carry
+
+        lax.fori_loop(0, meta_own[f, 3, 0], add_own, 0)
+
+
+def schur_kernel(acc, inverse, shared, out):
     local, half, width = acc.shape
     grids, levels = shared.shape[0], shared.shape[1]
-    rows = panel[...].reshape(local * half, BLOCK)
-    out[:, :, :BLOCK] = panel[...]
+
+    def panel_of(column):
+        return lax.dot_general(
+            column, inverse[...], NT, precision=HIGHEST, preferred_element_type=jnp.float32
+        )
+
+    rows = panel_of(acc[:, :, :BLOCK].reshape(local * half, BLOCK))
+    out[:, :, :BLOCK] = rows.reshape(local, half, BLOCK)
     for g in range(grids):
+        piece = panel_of(shared[g].reshape(levels * local * half, BLOCK))
+        prod = lax.dot_general(
+            rows, piece, NT, precision=HIGHEST, preferred_element_type=jnp.float32
+        ).reshape(local, half, levels * local * half)
         for lv in range(levels):
             for s in range(local):
                 if s == 0 and g == 0:
                     continue
-                prod = lax.dot_general(
-                    rows, shared[g, lv, s], NT, precision=HIGHEST,
-                    preferred_element_type=jnp.float32,
-                ).reshape(local, half, half)
                 lane = (s * grids + g) * BLOCK + lv * half
-                out[:, :, lane : lane + half] = acc[:, :, lane : lane + half] - prod
+                at = (lv * local + s) * half
+                out[:, :, lane : lane + half] = (
+                    acc[:, :, lane : lane + half] - prod[:, :, at : at + half]
+                )
 
 
 class Sends:
@@ -202,11 +199,11 @@
     sends = Sends(send_sems, recv_sems)
     locals_ = [
         pltpu.make_async_copy(own, out.at[front, grid, level], local_sems.at[0]),
-        pltpu.make_async_copy(meta, meta_own.at[front], local_sems.at[1]),
+        pltpu.make_async_copy(meta.at[front], meta_own.at[front], local_sems.at[1]),
     ]
     for copy in locals_:
         copy.start()
-    meta_z = [sends.start(meta, meta_own.at[front], at_front(f)) for f in order]
+    meta_z = [sends.start(meta.at[f], meta_own.at[front], at_front(f)) for f in order]
     panel_z = [sends.start(own, out.at[front, grid, level], at_front(f)) for f in order]
     to_x, to_y, to_core = [], [], []
 
@@ -289,7 +286,7 @@
             copy.wait_send()
 
 
-def share_kernel(own, out, send_sems, recv_sems, local_sem):
+def share_kernel(own, pivot, out, inverse, work, send_sems, recv_sems, local_sem):
     level, grid, across, along = plane_peers()
     corner = (across + 2) % 4
     x_peer, y_peer, core = {"grid": across}, {"grid": along}, {"lvl": 1 - level}
@@ -307,6 +304,13 @@
         to_y[local - 1 - r] = sends.start(own.at[local - 1 - r], place, y_peer)
     to_core.append(sends.start(own, out.at[grid, level], core))
     mine.start()
+    whole = pivot[...]
+    work[:, :BLOCK] = 0.5 * (whole + whole.T)
+    work[:, BLOCK:] = (
+        lax.broadcasted_iota(jnp.int32, (BLOCK, BLOCK), 0)
+        == lax.broadcasted_iota(jnp.int32, (BLOCK, BLOCK), 1)
+    ).astype(jnp.float32)
+    eliminate(work, inverse)
     to_x[0].wait_recv()
     half = out.at[across, level, 0]
     corner_y = sends.start(half, half, y_peer)
@@ -337,13 +341,6 @@
 SMEM = pl.BlockSpec(memory_space=pltpu.SMEM)
 
 
-def compact(codes, keep):
-    size = codes.shape[0]
-    position = jnp.cumsum(keep.astype(jnp.int32)) - 1
-    match = (position[None, :] == jnp.arange(size, dtype=jnp.int32)[:, None]) & keep[None, :]
-    return jnp.sum(jnp.where(match, codes[None, :], 0), axis=1), jnp.sum(keep.astype(jnp.int32))
-
-
 def owner_of(parents, parent_owner):
     ids = jnp.arange(parent_owner.shape[0], dtype=jnp.int32)
     return jnp.sum(jnp.where(parents[..., None] == ids, parent_owner, 0), axis=-1)
@@ -361,14 +358,22 @@
     row = tile_rows.reshape(slots)
     col = tile_cols.reshape(slots)
     live = (row * grids + me_g < child_blocks[0]) & (col < child_blocks[0])
-    to = jnp.where(live, owner_of(tile_parent.reshape(slots), parent_owner), -1)
-    meta = jnp.stack([row, col, to, tile_place.reshape(slots)])
+    to = owner_of(tile_parent.reshape(slots), parent_owner)
+    most = 2 * slots // fronts
+    sent = (to[None, :] == jnp.arange(fronts, dtype=jnp.int32)[:, None]) & live[None, :]
+    before = jnp.arange(slots)[:, None] < jnp.arange(slots)[None, :]
+    rank = jnp.sum(jnp.where(before[None] & sent[:, :, None], 1, 0), axis=1)
+    match = (rank[:, None, :] == jnp.arange(most, dtype=jnp.int32)[None, :, None]) & sent[:, None, :]
+    fields = jnp.stack([row, col, tile_place.reshape(slots), jnp.zeros_like(row)])
+    meta = jnp.sum(jnp.where(match[:, None], fields[None, :, None, :], 0), axis=3)
+    total = jnp.sum(sent.astype(jnp.int32), axis=1)[:, None, None]
+    meta = jnp.where(jnp.arange(4)[None, :, None] == 3, total, meta)
     gathered, meta_own, meta_pivot, raw_pivot = pl.pallas_call(
         gather_kernel,
         out_shape=(
             jax.ShapeDtypeStruct((fronts, grids, levels, local, half, depth), jnp.bfloat16),
-            jax.ShapeDtypeStruct((fronts, 4, slots), jnp.int32),
-            jax.ShapeDtypeStruct((levels, fronts, 4, slots), jnp.int32),
+            jax.ShapeDtypeStruct((fronts, 4, most), jnp.int32),
+            jax.ShapeDtypeStruct((levels, fronts, 4, most), jnp.int32),
             jax.ShapeDtypeStruct((levels, half, BLOCK), jnp.float32),
         ),
         in_specs=[VMEM, VMEM, VMEM],
@@ -383,45 +388,22 @@
         ),
         name="gather",
     )(rows_in[0], meta, parent_front[0, 0, 0, 0, :, :BLOCK])
-    raw_pivot = raw_pivot.reshape(levels * half, BLOCK)
-    own_rows = lax.dynamic_slice(
-        gathered, (0, me_g, me_l, 0, 0, 0), (fronts, 1, 1, local, half, depth)
-    ).reshape(fronts, local, half, depth)
-    child = jnp.arange(fronts, dtype=jnp.int32)[:, None] * (local * blocks)
-
-    def codes_of(m):
-        return child + m[:, 0] * blocks + m[:, 1]
-
-    mine = meta_own
-    own_list, own_count = compact(
-        (codes_of(mine) * 256 + mine[:, 3]).reshape(-1), (mine[:, 2] == me_f).reshape(-1)
-    )
-    lists, counts = [], [own_count]
-    for lv in range(levels):
-        m = meta_pivot[lv]
-        found, count = compact(
-            codes_of(m).reshape(-1), ((m[:, 2] == me_f) & (m[:, 3] == 0)).reshape(-1)
-        )
-        lists.append(found)
-        counts.append(count)
     parent = parent_front.reshape(parent_front.shape[1], half, parent_front.shape[5])
     return pl.pallas_call(
         assemble_kernel,
         out_shape=(
             jax.ShapeDtypeStruct(parent.shape, jnp.float32),
-            jax.ShapeDtypeStruct((parent.shape[0], half, BLOCK), jnp.float32),
+            jax.ShapeDtypeStruct((BLOCK, BLOCK), jnp.float32),
         ),
-        in_specs=[SMEM, SMEM, SMEM, VMEM, VMEM, VMEM, VMEM],
+        in_specs=[SMEM, SMEM, VMEM, VMEM, VMEM],
         out_specs=(VMEM, VMEM),
         scratch_shapes=[
             pltpu.VMEM((fronts * local * blocks, half, BLOCK), jnp.bfloat16),
             pltpu.VMEM((levels, fronts * local * blocks, half, BLOCK), jnp.bfloat16),
-            pltpu.VMEM((BLOCK, BLOCK), jnp.float32),
-            pltpu.VMEM((BLOCK, 2 * BLOCK), jnp.float32),
         ],
-        compiler_params=pltpu.CompilerParams(vmem_limit_bytes=52 * 1024 * 1024),
+        compiler_params=pltpu.CompilerParams(vmem_limit_bytes=30 * 1024 * 1024),
         name="assemble",
-    )(jnp.stack(counts), own_list, jnp.stack(lists), gathered, own_rows, parent, raw_pivot)
+    )(meta_own, meta_pivot, gathered, parent, raw_pivot)
 
 
 def exchange_tiles(
@@ -465,42 +447,41 @@
     )
     raw = lax.all_gather(assembled[0, :, :BLOCK][None], ("grid", "lvl"), axis=0, tiled=True)
     raw = raw[:levels].reshape(levels * half, BLOCK)
-    panel = pl.pallas_call(
-        tail_kernel,
-        out_shape=jax.ShapeDtypeStruct((parent_local, half, BLOCK), jnp.float32),
-        in_specs=[VMEM, VMEM],
-        out_specs=VMEM,
-        scratch_shapes=[pltpu.VMEM((BLOCK, 2 * BLOCK), jnp.float32)],
-        name="factor",
-    )(assembled, raw)
-    return assembled, panel
+    return assembled, raw
 
 
 def per_device(*args):
     levels, grids, fronts = lax.axis_size("lvl"), lax.axis_size("grid"), lax.axis_size("front")
     parent_front = args[-1]
-    assembled, panel = (gather_all if fronts == 4 else exchange_tiles)(*args)
-    shared = pl.pallas_call(
+    assembled, pivot = (gather_all if fronts == 4 else exchange_tiles)(*args)
+    column = assembled[:, :, :BLOCK]
+    shared, inverse = pl.pallas_call(
         share_kernel,
-        out_shape=jax.ShapeDtypeStruct((grids, levels) + panel.shape, jnp.float32),
-        in_specs=[VMEM],
-        out_specs=VMEM,
+        out_shape=(
+            jax.ShapeDtypeStruct((grids, levels) + column.shape, jnp.float32),
+            jax.ShapeDtypeStruct((BLOCK, BLOCK), jnp.float32),
+        ),
+        in_specs=[VMEM, VMEM],
+        out_specs=(VMEM, VMEM),
         scratch_shapes=[
+            pltpu.VMEM((BLOCK, 2 * BLOCK), jnp.float32),
             pltpu.SemaphoreType.DMA((12,)),
             pltpu.SemaphoreType.DMA((12,)),
             pltpu.SemaphoreType.DMA,
         ],
-        compiler_params=pltpu.CompilerParams(collective_id=1, has_side_effects=True),
+        compiler_params=pltpu.CompilerParams(
+            collective_id=1, has_side_effects=True, vmem_limit_bytes=16 * 1024 * 1024
+        ),
         name="share",
-    )(panel)
+    )(column, pivot)
     result = pl.pallas_call(
         schur_kernel,
         out_shape=jax.ShapeDtypeStruct(assembled.shape, jnp.float32),
         in_specs=[VMEM, VMEM, VMEM],
         out_specs=VMEM,
-        compiler_params=pltpu.CompilerParams(vmem_limit_bytes=32 * 1024 * 1024),
+        compiler_params=pltpu.CompilerParams(vmem_limit_bytes=20 * 1024 * 1024),
         name="schur",
-    )(assembled, panel, shared)
+    )(assembled, inverse, shared)
     return result.reshape(parent_front.shape)
 
 

time: 114 us -> 98.5 us (0.86)
  local copies, waits for them, and re-layouts: 10.5 us -> 3.55 us
  other arithmetic: 7.15 us -> 2.89 us
  Pallas kernels: 95.1 us -> 91.9 us
    pallas_call x1, Pallas kernels: 26.4 us -> 17.7 us  [gather_all(): pl.pallas_call(assemble_kernel, out_shape=(jax.ShapeDtypeStruct(parent.sh...]
    unnamed x12 -> x4, local copies, waits for them, and re-layouts: 6.47 us -> 2.53 us
    pallas_call x1, Pallas kernels: 15.2 us -> 19 us  [per_device(): pl.pallas_call(share_kernel, out_shape=(jax.ShapeDtypeStruct((grids, leve...]
    another operation x9 -> x1, other arithmetic: 3.66 us -> 0.76 us  [gather_all(): jnp.stack([row, col, tile_place.reshape(slots), jnp.zeros_like(row)])]
    pallas_call x1, Pallas kernels: 4.35 us -> 6.02 us  [per_device(): pl.pallas_call(schur_kernel, out_shape=jax.ShapeDtypeStruct(assembled.sha...]
    reshape x1 -> x0, local copies, waits for them, and re-layouts: 1.31 us -> none  [gather_all(): own_rows = lax.dynamic_slice(gathered, (0, me_g, me_l, 0, 0, 0), (fronts,...]
    convert_element_type x2 -> x0, other arithmetic: 1.29 us -> none  [compact(): keep.astype(jnp.int32)]
where the time goes in v3:
time: 98.5 us; the launch traced here: 99 us
  Pallas kernels  91.9 us (93%)
  local copies, waits for them, and re-layouts  3.55 us (4%)
  other arithmetic  2.89 us (3%)
    pallas_call x1, Pallas kernels, gather_all(): pl.pallas_call(gather_kernel, out_shape=(jax.ShapeDtypeStruct((fronts, gr...  49.1 us
    pallas_call x1, Pallas kernels, per_device(): pl.pallas_call(share_kernel, out_shape=(jax.ShapeDtypeStruct((grids, leve...  19 us
    pallas_call x1, Pallas kernels, gather_all(): pl.pallas_call(assemble_kernel, out_shape=(jax.ShapeDtypeStruct(parent.sh...  17.7 us
    pallas_call x1, Pallas kernels, per_device(): pl.pallas_call(schur_kernel, out_shape=jax.ShapeDtypeStruct(assembled.sha...  6.02 us
    unnamed x4, local copies, waits for them, and re-layouts  2.53 us

profile of v3, /device:TPU:9, one launch (start us, length us, event | category | flops | bytes accessed | tf_op | source)
XLA Modules:
  0.0 99.0 jit_solution(7726792231414355754)
XLA Ops:
  0.7 0.7 and_bitcast_fusion
  1.3 0.8 select_reduce_fusion.2
  2.1 0.1 convert_reduce_fusion
  2.2 0.1 pad.3.clone
  2.3 0.8 add_add_fusion
  3.1 0.1 select_reduce_fusion.1
  3.2 0.4 select_reduce_fusion
  3.6 0.1 broadcast_select_fusion.meta
  3.6 0.9 slice_bitcast_fusion.first
  4.6 0.0 copy-start.1
  4.6 0.9 copy-done.1
  5.5 49.1 %gather.1 = (bf16[4,4,2,2,128,512]{5,4,3,2,1,0:T(8,128)(2,1)S(1)}, s32[4,4,32]{2,1,0:T(4,128)S(1)}, s32[2,4,4,32]{3,2,1,0:T(4,128)S(1)}, f32[2,128,256]{2,1,0:T(8,128)S(1)}) custom-call(bf16[2,128,512]{2,1,0:T(8,128)(2,1)S(1)} %bitcast.17, s32[4,4,32]{2,1,0:T(4,128)S(1)} %broadcast_select_fusion.meta, f32[128,256]{1,0:T(8,128)S(1)} %slice_bitcast_fusion.first), custom_call_target="tpu_custom_call" | custom-call | tf_op jit(solution)/shard_map/gather/pallas_call | solution.py:371
  54.6 0.0 copy-start
  54.7 1.6 %copy-done = f32[1,2,1,1,128,2048]{5,4,3,2,1,0:T(8,128)S(1)} copy-done((f32[1,2,1,1,128,2048]{5,4,3,2,1,0:T(8,128)S(1)}, f32[1,2,1,1,128,2048]{5,4,3,2,1,0:T(8,128)}, u32[]{:S(2)}) %copy-start) | copy-done | bytes 2097176
  56.2 17.7 %assemble.1 = (f32[2,128,2048]{2,1,0:T(8,128)S(1)}, f32[256,256]{1,0:T(8,128)S(1)}) custom-call(s32[4,4,32]{2,1,0:T(4,128)S(1)} %get-tuple-element.13.meta_own, s32[2,4,4,32]{3,2,1,0:T(4,128)S(1)} %get-tuple-element.14.meta_pivot, bf16[4,4,2,2,128,512]{5,4,3,2,1,0:T(8,128)(2,1)S(1)} %get-tuple-element.15.gathered, f32[2,128,2048]{2,1,0:T(8,128)S(1)} %bitcast.16, ...), custom_call_target="tpu_custom_call" | custom-call | tf_op jit(solution)/shard_map/assemble/pallas_call | solution.py:392
  74.0 19.0 %share.1 = (f32[4,2,2,128,256]{4,3,2,1,0:T(8,128)S(1)}, f32[256,256]{1,0:T(8,128)S(1)}) custom-call(f32[2,128,256]{2,1,0:T(8,128)S(1)} %slice.7.own, f32[256,256]{1,0:T(8,128)S(1)} %get-tuple-element.18.pivot), custom_call_target="tpu_custom_call" | custom-call | tf_op jit(solution)/shard_map/share/pallas_call | solution.py:458
  93.0 6.0 %schur.1 = f32[2,128,2048]{2,1,0:T(8,128)} custom-call(f32[2,128,2048]{2,1,0:T(8,128)S(1)} %get-tuple-element.17.acc, f32[256,256]{1,0:T(8,128)S(1)} %get-tuple-element.19.inverse, f32[4,2,2,128,256]{4,3,2,1,0:T(8,128)S(1)} %get-tuple-element.20.shared), custom_call_target="tpu_custom_call" | custom-call | tf_op jit(solution)/shard_map/schur/pallas_call | solution.py:477
  (4 shorter events, 0.1 us)
Async XLA Ops:
  4.6 1.0 copy-start.1
  54.6 1.6 %copy-start = (f32[1,2,1,1,128,2048]{5,4,3,2,1,0:T(8,128)S(1)}, f32[1,2,1,1,128,2048]{5,4,3,2,1,0:T(8,128)}, u32[]{:S(2)}) copy-start(f32[1,2,1,1,128,2048]{5,4,3,2,1,0:T(8,128)} %param.15) | copy-start | bytes 6291460

commit v4 on v3

--- a/solution.py
+++ b/solution.py
@@ -15,7 +15,7 @@
 TN = (((0,), (0,)), ((), ()))
 
 
-def eliminate(work, inverse):
+def eliminate(work, inverse, begin, end):
     n = BLOCK
     row_ids = lax.broadcasted_iota(jnp.int32, (NB, 1), 0)
 
@@ -46,7 +46,7 @@
         work[: n - NB, :] = pltpu.roll(rest, 2 * n - NB, 1)
         return carry
 
-    lax.fori_loop(0, n // NB, step, 0)
+    lax.fori_loop(begin, end, step, 0)
 
 
 def assemble_kernel(
@@ -204,7 +204,8 @@
     for copy in locals_:
         copy.start()
     meta_z = [sends.start(meta.at[f], meta_own.at[front], at_front(f)) for f in order]
-    panel_z = [sends.start(own, out.at[front, grid, level], at_front(f)) for f in order]
+    panel_z = [sends.make(own, out.at[front, grid, level], at_front(f)) for f in order]
+    panel_z[0].start()
     to_x, to_y, to_core = [], [], []
 
     def spread(f, source):
@@ -266,7 +267,9 @@
         to_core.append(sends.start(place, place, core))
 
     for k in (1, 2, 3):
-        panel_z[k - 1].wait_recv()
+        panel_z[k - 1].wait()
+        if k < 3:
+            panel_z[k].start()
         place = out.at[planes[k], grid, level]
         spread(planes[k], place)
         forward(k - 1)
@@ -310,7 +313,7 @@
         lax.broadcasted_iota(jnp.int32, (BLOCK, BLOCK), 0)
         == lax.broadcasted_iota(jnp.int32, (BLOCK, BLOCK), 1)
     ).astype(jnp.float32)
-    eliminate(work, inverse)
+    eliminate(work, inverse, 0, 5)
     to_x[0].wait_recv()
     half = out.at[across, level, 0]
     corner_y = sends.start(half, half, y_peer)
@@ -324,6 +327,7 @@
     to_y[0].wait_recv()
     place = out.at[along, level]
     to_core.append(sends.start(place, place, core))
+    eliminate(work, inverse, 5, BLOCK // NB)
     corner_y.wait_recv()
     half = out.at[corner, level, 0]
     to_core.append(sends.start(half, half, core))

time: 98.5 us -> 100 us (1.015)
    pallas_call x1, Pallas kernels: 49.1 us -> 54.9 us  [gather_all(): pl.pallas_call(gather_kernel, out_shape=(jax.ShapeDtypeStruct((fronts, gr...]
    pallas_call x1, Pallas kernels: 19 us -> 14.7 us  [per_device(): pl.pallas_call(share_kernel, out_shape=(jax.ShapeDtypeStruct((grids, leve...]
where the time goes in v4:
time: 100 us; the launch traced here: 99.7 us
  Pallas kernels  92.5 us (92%)
  local copies, waits for them, and re-layouts  3.55 us (4%)
  other arithmetic  2.89 us (3%)
    pallas_call x1, Pallas kernels, gather_all(): pl.pallas_call(gather_kernel, out_shape=(jax.ShapeDtypeStruct((fronts, gr...  54.9 us
    pallas_call x1, Pallas kernels, gather_all(): pl.pallas_call(assemble_kernel, out_shape=(jax.ShapeDtypeStruct(parent.sh...  16.9 us
    pallas_call x1, Pallas kernels, per_device(): pl.pallas_call(share_kernel, out_shape=(jax.ShapeDtypeStruct((grids, leve...  14.7 us
    pallas_call x1, Pallas kernels, per_device(): pl.pallas_call(schur_kernel, out_shape=jax.ShapeDtypeStruct(assembled.sha...  6.02 us
    unnamed x4, local copies, waits for them, and re-layouts  2.53 us

profile of v4, /device:TPU:9, one launch (start us, length us, event | category | flops | bytes accessed | tf_op | source)
XLA Modules:
  0.0 99.7 jit_solution(15100203143774439553)
XLA Ops:
  0.7 0.7 and_bitcast_fusion
  1.3 0.8 select_reduce_fusion.2
  2.1 0.1 convert_reduce_fusion
  2.2 0.1 pad.3.clone
  2.3 0.8 add_add_fusion
  3.1 0.1 select_reduce_fusion.1
  3.2 0.4 select_reduce_fusion
  3.6 0.1 broadcast_select_fusion.meta
  3.6 0.9 slice_bitcast_fusion.first
  4.6 0.0 copy-start.1
  4.6 0.9 copy-done.1
  5.5 54.9 %gather.1 = (bf16[4,4,2,2,128,512]{5,4,3,2,1,0:T(8,128)(2,1)S(1)}, s32[4,4,32]{2,1,0:T(4,128)S(1)}, s32[2,4,4,32]{3,2,1,0:T(4,128)S(1)}, f32[2,128,256]{2,1,0:T(8,128)S(1)}) custom-call(bf16[2,128,512]{2,1,0:T(8,128)(2,1)S(1)} %bitcast.17, s32[4,4,32]{2,1,0:T(4,128)S(1)} %broadcast_select_fusion.meta, f32[128,256]{1,0:T(8,128)S(1)} %slice_bitcast_fusion.first), custom_call_target="tpu_custom_call" | custom-call | tf_op jit(solution)/shard_map/gather/pallas_call | solution.py:375
  60.5 0.0 copy-start
  60.5 1.6 %copy-done = f32[1,2,1,1,128,2048]{5,4,3,2,1,0:T(8,128)S(1)} copy-done((f32[1,2,1,1,128,2048]{5,4,3,2,1,0:T(8,128)S(1)}, f32[1,2,1,1,128,2048]{5,4,3,2,1,0:T(8,128)}, u32[]{:S(2)}) %copy-start) | copy-done | bytes 2097176
  62.1 16.9 %assemble.1 = (f32[2,128,2048]{2,1,0:T(8,128)S(1)}, f32[256,256]{1,0:T(8,128)S(1)}) custom-call(s32[4,4,32]{2,1,0:T(4,128)S(1)} %get-tuple-element.13.meta_own, s32[2,4,4,32]{3,2,1,0:T(4,128)S(1)} %get-tuple-element.14.meta_pivot, bf16[4,4,2,2,128,512]{5,4,3,2,1,0:T(8,128)(2,1)S(1)} %get-tuple-element.15.gathered, f32[2,128,2048]{2,1,0:T(8,128)S(1)} %bitcast.16, ...), custom_call_target="tpu_custom_call" | custom-call | tf_op jit(solution)/shard_map/assemble/pallas_call | solution.py:396
  79.0 14.7 %share.1 = (f32[4,2,2,128,256]{4,3,2,1,0:T(8,128)S(1)}, f32[256,256]{1,0:T(8,128)S(1)}) custom-call(f32[2,128,256]{2,1,0:T(8,128)S(1)} %slice.7.own, f32[256,256]{1,0:T(8,128)S(1)} %get-tuple-element.18.pivot), custom_call_target="tpu_custom_call" | custom-call | tf_op jit(solution)/shard_map/share/pallas_call | solution.py:462
  93.6 6.0 %schur.1 = f32[2,128,2048]{2,1,0:T(8,128)} custom-call(f32[2,128,2048]{2,1,0:T(8,128)S(1)} %get-tuple-element.17.acc, f32[256,256]{1,0:T(8,128)S(1)} %get-tuple-element.19.inverse, f32[4,2,2,128,256]{4,3,2,1,0:T(8,128)S(1)} %get-tuple-element.20.shared), custom_call_target="tpu_custom_call" | custom-call | tf_op jit(solution)/shard_map/schur/pallas_call | solution.py:481
  (4 shorter events, 0.1 us)
Async XLA Ops:
  4.6 1.0 copy-start.1
  60.5 1.6 %copy-start = (f32[1,2,1,1,128,2048]{5,4,3,2,1,0:T(8,128)S(1)}, f32[1,2,1,1,128,2048]{5,4,3,2,1,0:T(8,128)}, u32[]{:S(2)}) copy-start(f32[1,2,1,1,128,2048]{5,4,3,2,1,0:T(8,128)} %param.15) | copy-start | bytes 6291460

commit v5 on v4

--- a/solution.py
+++ b/solution.py
@@ -49,16 +49,12 @@
     lax.fori_loop(begin, end, step, 0)
 
 
-def assemble_kernel(
-    meta_own, meta_pivot, gathered, parent, raw_pivot, acc, pivot, tiles, pivot_tiles
-):
+def gram_of_child(f, gathered, tiles, pivot_tiles):
     fronts, grids, levels, local, half, depth = gathered.shape
     blocks = grids * local
     me_g, me_l = lax.axis_index("grid"), lax.axis_index("lvl")
-    most = meta_own.shape[2]
-
-    def gram(step, carry):
-        f, g = step // grids, step % grids
+
+    def gram(g, carry):
         right = gathered[f, g].reshape(levels * local * half, depth)
         left = jnp.concatenate(
             [
@@ -84,7 +80,15 @@
                         ]
         return carry
 
-    lax.fori_loop(0, fronts * grids, gram, 0)
+    lax.fori_loop(0, grids, gram, 0)
+
+
+def assemble_kernel(
+    meta_own, meta_pivot, tiles, pivot_tiles, parent, raw_pivot, acc, pivot
+):
+    fronts, local = meta_own.shape[0], parent.shape[0]
+    levels, half = pivot_tiles.shape[0], parent.shape[1]
+    blocks = tiles.shape[0] // (fronts * local)
     whole = [raw_pivot[lv] for lv in range(levels)]
     for lv in range(levels):
         rows = slice(lv * half, (lv + 1) * half)
@@ -184,7 +188,8 @@
 
 
 def gather_kernel(
-    own, meta, first, out, meta_own, meta_pivot, raw, send_sems, recv_sems, local_sems
+    own, meta, first, tiles, pivot_tiles, meta_own, meta_pivot, raw,
+    out, send_sems, recv_sems, local_sems,
 ):
     level, grid, across, along = plane_peers()
     corner = (across + 2) % 4
@@ -204,17 +209,17 @@
     for copy in locals_:
         copy.start()
     meta_z = [sends.start(meta.at[f], meta_own.at[front], at_front(f)) for f in order]
-    panel_z = [sends.make(own, out.at[front, grid, level], at_front(f)) for f in order]
-    panel_z[0].start()
-    to_x, to_y, to_core = [], [], []
-
-    def spread(f, source):
+    panel_z = [sends.start(own, out.at[front, grid, level], at_front(f)) for f in order]
+    to_x, to_y = [], []
+    landing = [[] for _ in range(4)]
+
+    def spread(k, f, source):
         place = out.at[f, grid, level]
         to_x.append(sends.start(source, place, x_peer))
         to_y.append(sends.start(source, place, y_peer))
-        to_core.append(sends.start(source, place, core))
-
-    spread(front, own)
+        landing[k].append(sends.start(source, place, core))
+
+    spread(0, front, own)
     planes = [front] + order
 
     raw_at = raw.at[level]
@@ -224,27 +229,6 @@
     raw_local = pltpu.make_async_copy(first, raw_at, local_sems.at[2])
     piv_local = pltpu.make_async_copy(meta_own, piv_at, local_sems.at[3])
 
-    locals_[1].wait()
-    for copy in meta_z:
-        copy.wait_recv()
-
-    @pl.when(grid == 0)
-    def _():
-        piv_local.start()
-        raw_local.start()
-        for copy in piv_copies + raw_copies:
-            copy.start()
-        piv_local.wait()
-        raw_local.wait()
-
-    for g in (1, 2, 3):
-
-        @pl.when(grid == g)
-        def _(g=g):
-            piv_copies[g - 1].wait_recv()
-            raw_copies[g - 1].wait_recv()
-
-    small = [sends.start(piv_at, piv_at, core), sends.start(raw_at, raw_at, core)]
     corners = []
 
     def forward(k):
@@ -253,33 +237,64 @@
         place = out.at[f, across, level]
         half = out.at[f, across, level, 0]
         corners.append(sends.start(half, half, y_peer))
-        to_core.append(sends.start(place, place, core))
+        landing[k].append(sends.start(place, place, core))
         to_y[k].wait_recv()
         place = out.at[f, along, level]
         half = out.at[f, along, level, 1]
         corners.append(sends.start(half, half, x_peer))
-        to_core.append(sends.start(place, place, core))
+        landing[k].append(sends.start(place, place, core))
 
     def corner_in(k):
         place = out.at[planes[k], corner, level]
         corners[2 * k].wait_recv()
         corners[2 * k + 1].wait_recv()
-        to_core.append(sends.start(place, place, core))
+        landing[k].append(sends.start(place, place, core))
+
+    def multiply(k):
+        if k == 0:
+            locals_[0].wait()
+        for copy in landing[k]:
+            copy.wait_recv()
+        gram_of_child(planes[k], out, tiles, pivot_tiles)
+
+    def small_out():
+        locals_[1].wait()
+        for copy in meta_z:
+            copy.wait_recv()
+
+        @pl.when(grid == 0)
+        def _():
+            piv_local.start()
+            raw_local.start()
+            for copy in piv_copies + raw_copies:
+                copy.start()
+            piv_local.wait()
+            raw_local.wait()
 
     for k in (1, 2, 3):
-        panel_z[k - 1].wait()
-        if k < 3:
-            panel_z[k].start()
+        panel_z[k - 1].wait_recv()
         place = out.at[planes[k], grid, level]
-        spread(planes[k], place)
+        spread(k, planes[k], place)
         forward(k - 1)
-        if k > 1:
+        if k == 1:
+            small_out()
+        else:
             corner_in(k - 2)
+            multiply(k - 2)
     forward(3)
     corner_in(2)
+    multiply(2)
     corner_in(3)
-    locals_[0].wait()
-    for copy in to_core + small:
+    for g in (1, 2, 3):
+
+        @pl.when(grid == g)
+        def _(g=g):
+            piv_copies[g - 1].wait_recv()
+            raw_copies[g - 1].wait_recv()
+
+    small = [sends.start(piv_at, piv_at, core), sends.start(raw_at, raw_at, core)]
+    multiply(3)
+    for copy in small:
         copy.wait_recv()
     sends.finish()
 
@@ -372,23 +387,25 @@
     meta = jnp.sum(jnp.where(match[:, None], fields[None, :, None, :], 0), axis=3)
     total = jnp.sum(sent.astype(jnp.int32), axis=1)[:, None, None]
     meta = jnp.where(jnp.arange(4)[None, :, None] == 3, total, meta)
-    gathered, meta_own, meta_pivot, raw_pivot = pl.pallas_call(
+    tiles, pivot_tiles, meta_own, meta_pivot, raw_pivot = pl.pallas_call(
         gather_kernel,
         out_shape=(
-            jax.ShapeDtypeStruct((fronts, grids, levels, local, half, depth), jnp.bfloat16),
+            jax.ShapeDtypeStruct((fronts * local * blocks, half, BLOCK), jnp.bfloat16),
+            jax.ShapeDtypeStruct((levels, fronts * local * blocks, half, BLOCK), jnp.bfloat16),
             jax.ShapeDtypeStruct((fronts, 4, most), jnp.int32),
             jax.ShapeDtypeStruct((levels, fronts, 4, most), jnp.int32),
             jax.ShapeDtypeStruct((levels, half, BLOCK), jnp.float32),
         ),
         in_specs=[VMEM, VMEM, VMEM],
-        out_specs=(VMEM, VMEM, VMEM, VMEM),
+        out_specs=(VMEM, VMEM, VMEM, VMEM, VMEM),
         scratch_shapes=[
+            pltpu.VMEM((fronts, grids, levels, local, half, depth), jnp.bfloat16),
             pltpu.SemaphoreType.DMA((64,)),
             pltpu.SemaphoreType.DMA((64,)),
             pltpu.SemaphoreType.DMA((4,)),
         ],
         compiler_params=pltpu.CompilerParams(
-            collective_id=0, has_side_effects=True, vmem_limit_bytes=24 * 1024 * 1024
+            collective_id=0, has_side_effects=True, vmem_limit_bytes=32 * 1024 * 1024
         ),
         name="gather",
     )(rows_in[0], meta, parent_front[0, 0, 0, 0, :, :BLOCK])
@@ -399,15 +416,11 @@
             jax.ShapeDtypeStruct(parent.shape, jnp.float32),
             jax.ShapeDtypeStruct((BLOCK, BLOCK), jnp.float32),
         ),
-        in_specs=[SMEM, SMEM, VMEM, VMEM, VMEM],
+        in_specs=[SMEM, SMEM, VMEM, VMEM, VMEM, VMEM],
         out_specs=(VMEM, VMEM),
-        scratch_shapes=[
-            pltpu.VMEM((fronts * local * blocks, half, BLOCK), jnp.bfloat16),
-            pltpu.VMEM((levels, fronts * local * blocks, half, BLOCK), jnp.bfloat16),
-        ],
-        compiler_params=pltpu.CompilerParams(vmem_limit_bytes=30 * 1024 * 1024),
+        compiler_params=pltpu.CompilerParams(vmem_limit_bytes=24 * 1024 * 1024),
         name="assemble",
-    )(meta_own, meta_pivot, gathered, parent, raw_pivot)
+    )(meta_own, meta_pivot, tiles, pivot_tiles, parent, raw_pivot)
 
 
 def exchange_tiles(

time: 100 us -> 92.2 us (0.922)
  the two profiles are of different devices: /device:TPU:9 before, /device:TPU:0 now
where the time goes in v5:
time: 92.2 us; the launch traced here: 91.5 us
  Pallas kernels  84.3 us (91%)
  local copies, waits for them, and re-layouts  3.55 us (4%)
  other arithmetic  2.89 us (3%)
    pallas_call x1, Pallas kernels, gather_all(): pl.pallas_call(gather_kernel, out_shape=(jax.ShapeDtypeStruct((fronts * l...  56.1 us
    pallas_call x1, Pallas kernels, per_device(): pl.pallas_call(share_kernel, out_shape=(jax.ShapeDtypeStruct((grids, leve...  18.1 us
    pallas_call x1, Pallas kernels, per_device(): pl.pallas_call(schur_kernel, out_shape=jax.ShapeDtypeStruct(assembled.sha...  6.02 us
    pallas_call x1, Pallas kernels, gather_all(): pl.pallas_call(assemble_kernel, out_shape=(jax.ShapeDtypeStruct(parent.sh...  4.15 us
    unnamed x4, local copies, waits for them, and re-layouts  2.53 us

profile of v5, /device:TPU:0, one launch (start us, length us, event | category | flops | bytes accessed | tf_op | source)
XLA Modules:
  0.0 91.5 jit_solution(12900041912506559859)
XLA Ops:
  0.7 0.7 and_bitcast_fusion
  1.3 0.8 select_reduce_fusion.2
  2.1 0.1 convert_reduce_fusion
  2.2 0.1 pad.3.clone
  2.3 0.8 add_add_fusion
  3.1 0.1 select_reduce_fusion.1
  3.2 0.4 select_reduce_fusion
  3.6 0.1 broadcast_select_fusion.meta
  3.6 0.9 %slice_bitcast_fusion.first = f32[128,256]{1,0:T(8,128)S(1)} fusion(f32[1,2,1,1,128,2048]{5,4,3,2,1,0:T(8,128)} %param.15), kind=kLoop, calls=%fused_computation.1 | loop fusion | bytes 262144 | tf_op jit(solution)/shard_map/squeeze | solution.py:411
  4.6 0.0 copy-start.1
  4.6 0.9 %copy-done.1 = bf16[1,2,1,1,128,512]{5,4,3,2,1,0:T(8,128)(2,1)S(1)} copy-done((bf16[1,2,1,1,128,512]{5,4,3,2,1,0:T(8,128)(2,1)S(1)}, bf16[1,2,1,1,128,512]{5,4,3,2,1,0:T(8,128)(2,1)}, u32[]{:S(2)}) %copy-start.1) | copy-done | bytes 262168
  5.5 56.1 %gather.1 = (bf16[64,128,256]{2,1,0:T(8,128)(2,1)S(1)}, bf16[2,64,128,256]{3,2,1,0:T(8,128)(2,1)S(1)}, s32[4,4,32]{2,1,0:T(4,128)S(1)}, s32[2,4,4,32]{3,2,1,0:T(4,128)S(1)}, f32[2,128,256]{2,1,0:T(8,128)S(1)}) custom-call(bf16[2,128,512]{2,1,0:T(8,128)(2,1)S(1)} %bitcast.17, s32[4,4,32]{2,1,0:T(4,128)S(1)} %broadcast_select_fusion.meta, ...), custom_call_target="tpu_custom_call" | custom-call | tf_op jit(solution)/shard_map/gather/pallas_call | solution.py:390
  61.6 0.0 copy-start
  61.6 1.6 %copy-done = f32[1,2,1,1,128,2048]{5,4,3,2,1,0:T(8,128)S(1)} copy-done((f32[1,2,1,1,128,2048]{5,4,3,2,1,0:T(8,128)S(1)}, f32[1,2,1,1,128,2048]{5,4,3,2,1,0:T(8,128)}, u32[]{:S(2)}) %copy-start) | copy-done | bytes 2097176
  63.2 4.1 %assemble.1 = (f32[2,128,2048]{2,1,0:T(8,128)S(1)}, f32[256,256]{1,0:T(8,128)S(1)}) custom-call(s32[4,4,32]{2,1,0:T(4,128)S(1)} %get-tuple-element.14.meta_own, s32[2,4,4,32]{3,2,1,0:T(4,128)S(1)} %get-tuple-element.15.meta_pivot, bf16[64,128,256]{2,1,0:T(8,128)(2,1)S(1)} %get-tuple-element.16.tiles, ...), custom_call_target="tpu_custom_call" | custom-call | tf_op jit(solution)/shard_map/assemble/pallas_call | solution.py:413
  67.4 18.1 %share.1 = (f32[4,2,2,128,256]{4,3,2,1,0:T(8,128)S(1)}, f32[256,256]{1,0:T(8,128)S(1)}) custom-call(f32[2,128,256]{2,1,0:T(8,128)S(1)} %slice.7.own, f32[256,256]{1,0:T(8,128)S(1)} %get-tuple-element.20.pivot), custom_call_target="tpu_custom_call" | custom-call | tf_op jit(solution)/shard_map/share/pallas_call | solution.py:475
  85.5 6.0 %schur.1 = f32[2,128,2048]{2,1,0:T(8,128)} custom-call(f32[2,128,2048]{2,1,0:T(8,128)S(1)} %get-tuple-element.19.acc, f32[256,256]{1,0:T(8,128)S(1)} %get-tuple-element.21.inverse, f32[4,2,2,128,256]{4,3,2,1,0:T(8,128)S(1)} %get-tuple-element.22.shared), custom_call_target="tpu_custom_call" | custom-call | tf_op jit(solution)/shard_map/schur/pallas_call | solution.py:494
  (4 shorter events, 0.1 us)
Async XLA Ops:
  4.6 1.0 %copy-start.1 = (bf16[1,2,1,1,128,512]{5,4,3,2,1,0:T(8,128)(2,1)S(1)}, bf16[1,2,1,1,128,512]{5,4,3,2,1,0:T(8,128)(2,1)}, u32[]{:S(2)}) copy-start(bf16[1,2,1,1,128,512]{5,4,3,2,1,0:T(8,128)(2,1)} %param.8) | copy-start | bytes 786436
  61.6 1.6 %copy-start = (f32[1,2,1,1,128,2048]{5,4,3,2,1,0:T(8,128)S(1)}, f32[1,2,1,1,128,2048]{5,4,3,2,1,0:T(8,128)}, u32[]{:S(2)}) copy-start(f32[1,2,1,1,128,2048]{5,4,3,2,1,0:T(8,128)} %param.15) | copy-start | bytes 6291460
